TPU v7x, 128 devices: a whole 4x4x4 slice. The times are simulated.
128 devices in a mesh: rows: 8 (over y_lo, z), cols: 16 (over y_hi, x, core).
Axes of the slice: x: 4, y: 4 (y_hi: 2, y_lo: 2; y = y_hi * 2 + y_lo), z: 4, core: 2. Of those that a mesh axis runs over, the one named last changes fastest.
Arguments:
- frames: bfloat16 [4, 2048, 2048], P(None, 'rows', 'cols'), may hold values from -6 to 6
- enc_taps: float32 [9, 32], replicated, may hold values from -2 to 2
- enc_bias: float32 [32], replicated, may hold values from -3 to 3
- enc_proj: bfloat16 [512, 32], replicated, may hold values from -0.25 to 0.25
- w_in: bfloat16 [128, 512], replicated, may hold values from -0.5 to 0.5
- b_in: float32 [512], replicated, may hold values from -3 to 3
- ln_gain: float32 [512], replicated, may hold values from 0.1 to 1.9
- ln_bias: float32 [512], replicated, may hold values from -3 to 3
- spec_w1: float32 [2, 8, 64, 64], replicated, may hold values from -0.5 to 0.5
- spec_b1: float32 [2, 512], replicated, may hold values from -3 to 3
- spec_w2: float32 [2, 8, 64, 64], replicated, may hold values from -0.5 to 0.5
- spec_b2: float32 [2, 512], replicated, may hold values from -3 to 3
- cotangent: bfloat16 [512, 512, 512], P(('rows', 'cols')), may hold values from -6 to 6
Outputs:
- denoised: bfloat16 [512, 512, 512], P(('rows', 'cols'))
- grad_w_in: float32 [128, 512], replicated
- grad_b_in: float32 [512], replicated
- grad_ln_gain: float32 [512], replicated
- grad_ln_bias: float32 [512], replicated
- grad_w1: float32 [2, 8, 64, 64], replicated
- grad_b1: float32 [2, 512], replicated
- grad_w2: float32 [2, 8, 64, 64], replicated
- grad_b2: float32 [2, 512], replicated
All inputs are finite; a program needn't handle non-finite values.
Results may differ from a plain program's by a relative error of at most 0.0039.
The roundings to bfloat16 on the way count: a program that leaves them out, or rounds other values in their place, can miss the bound.
Values may be sent and summed in bfloat16 or wider, within the bound.
A program may use at most 128 MiB of HBM per device.

v0:
```python
import math

import jax
import jax.numpy as jnp
from jax import lax
from jax.sharding import PartitionSpec as P

KH = 128
KW_DEV = 1


epsilon = 1e-05
highest = lax.Precision.HIGHEST


def extended(value, sides, width):
    for axis, dim in sides:
        size, length = (lax.axis_size(axis), value.shape[dim])
        up = [(i, (i + 1) % size) for i in range(size - 1)]
        down = [(j, i) for i, j in up]
        last = lax.slice_in_dim(value, length - width, length, axis=dim)
        initial = lax.slice_in_dim(value, 0, width, axis=dim)
        before = lax.ppermute(last, axis, up)
        after = lax.ppermute(initial, axis, down)
        value = jnp.concatenate([before, value, after], axis=dim)
    return value


def width_tables(frequency, count):
    cell_index = jnp.arange(count, dtype=jnp.int32)
    angles = (
        2.0
        * math.pi
        / count
        * jnp.mod(frequency[:, None] * cell_index[None, :], count).astype(jnp.float32)
    )
    forward = jnp.stack([jnp.cos(angles), -jnp.sin(angles)])
    weights = jnp.where(frequency == 0, 1.0, 2.0).astype(jnp.float32)
    return (forward.astype(jnp.bfloat16), (forward * weights[None, :, None]).astype(jnp.bfloat16))


def height_table(cell_index, modes, count):
    frequency = jnp.arange(modes, dtype=jnp.int32) - modes // 2
    angles = (
        2.0
        * math.pi
        / count
        * jnp.mod(frequency[:, None] * cell_index[None, :], count).astype(jnp.float32)
    )
    cosine = jnp.cos(angles)
    sine_table = jnp.sin(angles)
    first = jnp.stack([cosine, sine_table], axis=-1)
    second = jnp.stack([-sine_table, cosine], axis=-1)
    return jnp.concatenate([first, second], axis=0).astype(jnp.bfloat16)


def conv_project(padded, enc_taps, enc_bias, patch_proj):
    height = padded.shape[0] - 2
    breadth = padded.shape[1] - 2
    values = padded.astype(jnp.float32)
    hidden = jnp.broadcast_to(enc_bias[:, None, None], (enc_taps.shape[1], height, breadth))
    for tap_index in range(9):
        offset_down = tap_index // 3
        offset_side = tap_index % 3
        hidden = (
            hidden
            + enc_taps[tap_index][:, None, None]
            * values[None, offset_down : offset_down + height, offset_side : offset_side + breadth]
        )
    hidden = jnp.maximum(hidden, 0.0).astype(jnp.bfloat16)
    blocks = hidden.reshape(hidden.shape[0], height // 4, 4, breadth // 4, 4)
    return jnp.einsum("caybx,cyxo->abo", blocks, patch_proj, preferred_element_type=jnp.float32)


def embed(latent, w_in, b_in, ln_gain, ln_bias):
    flat = latent.reshape(-1, latent.shape[-1])
    embedded = (jnp.dot(flat, w_in, preferred_element_type=jnp.float32) + b_in).reshape(
        latent.shape[0], latent.shape[1], -1
    )
    average = jnp.mean(embedded, axis=-1, keepdims=True)
    centered = embedded - average
    inverse_std = lax.rsqrt(jnp.mean(centered * centered, axis=-1, keepdims=True) + epsilon)
    normalized = centered * inverse_std
    normed = (normalized * ln_gain + ln_bias).astype(jnp.bfloat16)
    return (embedded, normalized, inverse_std, normed)


def complex_block(real_part, imag_part, weight):

    def times_block(values, matrix):
        return jnp.einsum("mbi,bio->mbo", values, matrix, precision=highest)

    return (
        times_block(real_part, weight[0]) - times_block(imag_part, weight[1]),
        times_block(real_part, weight[1]) + times_block(imag_part, weight[0]),
    )


def complex_back(real_part, imag_part, grad_real, grad_imag, weight):

    def transposed(values, matrix):
        return jnp.einsum("mbo,bio->mbi", values, matrix, precision=highest)

    def outer_sum(left, right):
        return jnp.einsum("mbi,mbo->bio", left, right, precision=highest)

    in_real = transposed(grad_real, weight[0]) + transposed(grad_imag, weight[1])
    in_imag = transposed(grad_imag, weight[0]) - transposed(grad_real, weight[1])
    grad_weight = jnp.stack(
        [
            outer_sum(real_part, grad_real) + outer_sum(imag_part, grad_imag),
            outer_sum(real_part, grad_imag) - outer_sum(imag_part, grad_real),
        ]
    )
    return (in_real, in_imag, grad_weight)


def spectral_forward(coeffs, spec_w1, spec_b1, spec_w2, spec_b2):
    blocks = spec_w1.shape[1]
    block_size = spec_w1.shape[2]
    real_part = coeffs[0].reshape(-1, blocks, block_size)
    imag_part = coeffs[1].reshape(-1, blocks, block_size)
    pre_real, pre_imag = complex_block(real_part, imag_part, spec_w1)
    pre_real = pre_real + spec_b1[0].reshape(blocks, block_size)
    pre_imag = pre_imag + spec_b1[1].reshape(blocks, block_size)
    act_real = jax.nn.gelu(pre_real)
    act_imag = jax.nn.gelu(pre_imag)
    out_real, out_imag = complex_block(act_real, act_imag, spec_w2)
    out_real = out_real + spec_b2[0].reshape(blocks, block_size)
    out_imag = out_imag + spec_b2[1].reshape(blocks, block_size)
    mixed_modes = jnp.stack([out_real, out_imag]).reshape(coeffs.shape)
    return (mixed_modes, (real_part, imag_part, pre_real, pre_imag, act_real, act_imag))


def spectral_backward(stored, grad_modes, spec_w1, spec_w2):
    real_part, imag_part, pre_real, pre_imag, act_real, act_imag = stored
    blocks = spec_w1.shape[1]
    block_size = spec_w1.shape[2]
    grad_real = grad_modes[0].reshape(-1, blocks, block_size)
    grad_imag = grad_modes[1].reshape(-1, blocks, block_size)
    grad_b2 = jnp.stack(
        [jnp.sum(grad_real, axis=0).reshape(-1), jnp.sum(grad_imag, axis=0).reshape(-1)]
    )
    back_real, back_imag, grad_w2 = complex_back(act_real, act_imag, grad_real, grad_imag, spec_w2)
    back_real = jax.vjp(jax.nn.gelu, pre_real)[1](back_real)[0]
    back_imag = jax.vjp(jax.nn.gelu, pre_imag)[1](back_imag)[0]
    grad_b1 = jnp.stack(
        [jnp.sum(back_real, axis=0).reshape(-1), jnp.sum(back_imag, axis=0).reshape(-1)]
    )
    in_real, in_imag, grad_w1 = complex_back(real_part, imag_part, back_real, back_imag, spec_w1)
    grad_coeffs = jnp.stack([in_real, in_imag]).reshape(grad_modes.shape)
    return (grad_coeffs, grad_w1, grad_b1, grad_w2, grad_b2)


def toward_modes(values):
    return lax.all_to_all(values, ("rows", "cols"), split_axis=2, concat_axis=0, tiled=True)


def toward_rows(values):
    return lax.all_to_all(values, ("rows", "cols"), split_axis=0, concat_axis=2, tiled=True)


def body(
    frames,
    enc_taps,
    enc_bias,
    enc_proj,
    w_in,
    b_in,
    ln_gain,
    ln_bias,
    spec_w1,
    spec_b1,
    spec_w2,
    spec_b2,
    cotangent,
):
    row_count = lax.axis_size("rows")
    col_count = lax.axis_size("cols")
    padded = extended(frames, (("rows", 1), ("cols", 2)), 1)
    patch_proj = enc_proj.reshape(enc_taps.shape[1], 4, 4, -1)
    parts = [
        conv_project(padded[frame_index], enc_taps, enc_bias, patch_proj)
        for frame_index in range(frames.shape[0])
    ]
    latent = jnp.concatenate(parts, axis=-1).astype(jnp.bfloat16)
    latent = lax.all_to_all(latent, "cols", split_axis=0, concat_axis=1, tiled=True)
    side = latent.shape[1]
    channels = cotangent.shape[2]
    modes = KW_DEV * row_count * col_count
    factor = side ** (-0.5)
    natural_cells = jnp.arange(side, dtype=jnp.int32)
    natural_modes = jnp.arange(modes, dtype=jnp.int32)
    wave_fwd, wave_inv = width_tables(natural_modes, side)
    placed_fwd, placed_inv = width_tables(natural_modes, side)
    rotation = height_table(natural_cells, KH, side)
    placed_rotation = height_table(natural_cells, KH, side)
    embedded, normalized, inverse_std, normed = embed(latent, w_in, b_in, ln_gain, ln_bias)
    spectrum = (
        jnp.einsum("pkn,hnc->hpkc", wave_fwd, normed, preferred_element_type=jnp.float32) * factor
    ).astype(jnp.bfloat16)
    grad_grid = (
        jnp.einsum("pkn,hnc->hpkc", wave_inv, cotangent, preferred_element_type=jnp.float32)
        * factor
    ).astype(jnp.bfloat16)
    spectrum = toward_modes(spectrum)
    coeffs = (
        jnp.einsum("qhp,hpkc->qkc", placed_rotation, spectrum, preferred_element_type=jnp.float32)
        * factor
    )
    coeffs = coeffs.reshape(2, KH, KW_DEV, channels)
    mixed_modes, stored = spectral_forward(coeffs, spec_w1, spec_b1, spec_w2, spec_b2)
    modes_bf = mixed_modes.astype(jnp.bfloat16).reshape(2 * KH, KW_DEV, channels)
    grid_back = (
        jnp.einsum("qhp,qkc->hpkc", rotation, modes_bf, preferred_element_type=jnp.float32) * factor
    ).astype(jnp.bfloat16)
    grid_back = toward_rows(grid_back)
    grad_grid = toward_modes(grad_grid)
    grad_modes = (
        jnp.einsum("qhp,hpkc->qkc", placed_rotation, grad_grid, preferred_element_type=jnp.float32)
        * factor
    )
    grad_modes = grad_modes.reshape(2, KH, KW_DEV, channels)
    grad_coeffs, grad_w1, grad_b1, grad_w2, grad_b2 = spectral_backward(
        stored, grad_modes, spec_w1, spec_w2
    )
    coeffs_bf = grad_coeffs.astype(jnp.bfloat16).reshape(2 * KH, KW_DEV, channels)
    grad_cells = (
        jnp.einsum("qhp,qkc->hpkc", rotation, coeffs_bf, preferred_element_type=jnp.float32)
        * factor
    ).astype(jnp.bfloat16)
    grad_cells = toward_rows(grad_cells)
    branch = (
        jnp.einsum("pkn,hpkc->hnc", placed_inv, grid_back, preferred_element_type=jnp.float32)
        * factor
    )
    denoised = (embedded + branch).astype(jnp.bfloat16)
    grad_normed = (
        jnp.einsum("pkn,hpkc->hnc", placed_fwd, grad_cells, preferred_element_type=jnp.float32)
        * factor
    )
    grad_ln_gain = jnp.sum(grad_normed * normalized, axis=(0, 1))
    grad_ln_bias = jnp.sum(grad_normed, axis=(0, 1))
    scaled = grad_normed * ln_gain
    grad_embedded = cotangent.astype(jnp.float32) + inverse_std * (
        scaled
        - jnp.mean(scaled, axis=-1, keepdims=True)
        - normalized * jnp.mean(scaled * normalized, axis=-1, keepdims=True)
    )
    grad_b_in = jnp.sum(grad_embedded, axis=(0, 1))
    grad_bf = grad_embedded.astype(jnp.bfloat16).reshape(-1, channels)
    grad_w_in = jnp.einsum(
        "mi,mc->ic",
        latent.reshape(-1, latent.shape[-1]),
        grad_bf,
        preferred_element_type=jnp.float32,
    )
    grad_w_in, grad_b_in, grad_ln_gain, grad_ln_bias, grad_w1, grad_b1, grad_w2, grad_b2 = lax.psum(
        (grad_w_in, grad_b_in, grad_ln_gain, grad_ln_bias, grad_w1, grad_b1, grad_w2, grad_b2),
        ("rows", "cols"),
    )
    return (
        denoised,
        grad_w_in,
        grad_b_in,
        grad_ln_gain,
        grad_ln_bias,
        grad_w1,
        grad_b1,
        grad_w2,
        grad_b2,
    )


def solution(mesh):
    return jax.shard_map(
        body,
        mesh=mesh,
        in_specs=(
            P(None, "rows", "cols"),
            P(),
            P(),
            P(),
            P(),
            P(),
            P(),
            P(),
            P(),
            P(),
            P(),
            P(),
            P(("rows", "cols"), None, None),
        ),
        out_specs=(P(("rows", "cols"), None, None), P(), P(), P(), P(), P(), P(), P(), P()),
        check_vma=False,
    )
```

profile of v0, /device:TPU:1, one launch (start us, length us, event | category | flops | bytes accessed | tf_op | source)
XLA Modules:
  0.0 763.0 jit_solution(10789933033633023939)
XLA Ops:
  31.3 6.2 mul.863
  42.0 5.7 mul.868
  52.2 5.7 mul.873
  62.4 5.7 mul.878
  72.6 5.7 mul.883
  82.8 5.9 mul.888
  93.2 5.7 mul.893
  103.4 5.7 mul.898
  113.7 5.7 mul.903
  123.9 5.7 mul.906
  134.1 5.9 mul.909
  144.5 5.7 mul.912
  154.7 5.7 mul.915
  165.0 5.7 mul.918
  175.2 5.7 mul.921
  185.4 6.1 mul.924
  196.0 5.7 mul.927
  206.2 5.7 mul.930
  216.9 5.7 mul.933
  227.2 5.7 mul.936
  237.4 5.9 mul.939
  247.8 5.7 mul.942
  258.0 5.7 mul.945
  268.2 5.7 mul.948
  278.4 5.7 mul.951
  288.6 6.1 mul.954
  299.2 5.7 mul.957
  309.5 5.7 mul.960
  319.7 5.7 mul.963
  329.9 5.7 mul.966
  340.1 5.9 mul.969
  350.5 5.7 mul.972
  360.7 5.7 mul.975
  370.9 5.7 mul.978
  391.4 5.7 mul.984
  402.3 5.7 fusion.34
  408.2 5.9 fusion.35
  414.3 6.1 fusion.36
  420.5 5.9 fusion.37
  428.7 9.4 %all-to-all-start = ((bf16[64,32,128]{2,1,0:T(8,128)(2,1)}), bf16[64,32,128]{2,1,0:T(8,128)(2,1)S(1)}, u32[]{:S(2)}, u32[]{:S(2)}) async-start(bf16[64,32,128]{2,1,0:T(8,128)(2,1)} %copy.299), calls=%async_computation | async-start | bytes 1048576 | tf_op jit(solution)/shard_map/all_to_all | solution.py:187
  449.9 11.0 %all-to-all-start.3 = ((bf16[4,2,128,512]{3,0,1,2:T(4,128)(2,1)}), bf16[4,2,128,512]{3,0,1,2:T(4,128)(2,1)S(1)}, u32[]{:S(2)}, u32[]{:S(2)}) async-start(bf16[4,2,128,512]{3,0,1,2:T(4,128)(2,1)} %copy.316), calls=%async_computation.3 | async-start | bytes 2097152 | tf_op jit(solution)/shard_map/all_to_all | solution.py:156
  484.0 10.2 %all-to-all-start.1 = ((bf16[4,2,128,512]{3,1,0,2:T(2,128)(2,1)}), bf16[4,2,128,512]{3,1,0,2:T(2,128)(2,1)}, u32[]{:S(2)}, u32[]{:S(2)}) async-start(bf16[4,2,128,512]{3,1,0,2:T(2,128)(2,1)} %copy.302), calls=%async_computation.1 | async-start | bytes 2097152 | tf_op jit(solution)/shard_map/all_to_all | solution.py:156
  505.5 7.5 all-to-all-done.1
  549.1 5.9 all-to-all-start.4
  573.8 9.3 %all-to-all-start.2 = ((bf16[512,2,1,512]{3,1,2,0:T(2,128)(2,1)}), bf16[512,2,1,512]{3,1,2,0:T(2,128)(2,1)}, u32[]{:S(2)}, u32[]{:S(2)}) async-start(bf16[512,2,1,512]{3,1,2,0:T(2,128)(2,1)} %copy.312), calls=%async_computation.2 | async-start | bytes 2097152 | tf_op jit(solution)/shard_map/all_to_all | solution.py:160
  595.8 6.0 all-to-all-done.2
  612.5 64.3 %all-reduce = (f32[512]{0:T(512)}, f32[512]{0:T(512)}, f32[512]{0:T(512)}, f32[2,512]{1,0:T(2,128)}, f32[2,512]{1,0:T(2,128)}) all-reduce(f32[512]{0:T(512)S(1)} %copy-done.71, f32[512]{0:T(512)S(1)} %copy-done.70, f32[512]{0:T(512)S(1)} %fusion.10, f32[2,512]{1,0:T(2,128)S(1)} %copy-done.69, ...), channel_id=1, replica_groups=mesh['rows'=8,'cols'=16] {'rows','cols'}, use_global_device_ids=true, to_apply=%region_6.7 | all-reduce | flops 3584 | bytes 28672 | tf_op jit(solution)/shard_map/psum | solution.py:258
  676.7 73.8 %all-reduce.4.cloned.1.call-done = (f32[128,512]{1,0:T(8,128)}, f32[2,8,64,64]{3,2,1,0:T(8,128)}, f32[2,8,64,64]{3,2,1,0:T(8,128)}) async-done(((f32[128,512]{1,0:T(8,128)}, f32[2,8,64,64]{3,2,1,0:T(8,128)}, f32[2,8,64,64]{3,2,1,0:T(8,128)}), (f32[128,512]{1,0:T(8,128)}, f32[2,8,64,64]{3,2,1,0:T(8,128)}, f32[2,8,64,64]{3,2,1,0:T(8,128)})) %all-reduce.4.cloned.1.call-update) | async-done | bytes 786448 | tf_op jit(solution)/shard_map/psum | solution.py:258
  (305 shorter events, 325.3 us)
Async XLA Ops:
  7.2 455.6 %copy-start = (bf16[128,512]{1,0:T(8,128)(2,1)S(1)}, bf16[128,512]{1,0:T(8,128)(2,1)}, u32[]{:S(2)}) copy-start(bf16[128,512]{1,0:T(8,128)(2,1)} %param.17) | copy-start | bytes 393220
  7.2 11.1 %copy-start.21 = (bf16[4,256,128]{2,1,0:T(8,128)(2,1)S(1)}, bf16[4,256,128]{2,1,0:T(8,128)(2,1)}, u32[]{:S(2)}) copy-start(bf16[4,256,128]{2,1,0:T(8,128)(2,1)} %param.13) | copy-start | bytes 786436
  7.2 11.1 %copy-start.74 = (f32[9,32]{1,0:T(8,128)S(1)}, f32[9,32]{1,0:T(8,128)}, u32[]{:S(2)}) copy-start(f32[9,32]{1,0:T(8,128)} %param.14) | copy-start | bytes 3460
  7.2 17.2 %copy-start.73 = (f32[2,512]{1,0:T(2,128)S(1)}, f32[2,512]{1,0:T(2,128)}, u32[]{:S(2)}) copy-start(f32[2,512]{1,0:T(2,128)} %param.22) | copy-start | bytes 12292
  7.2 17.2 %copy-start.72 = (f32[2,512]{1,0:T(2,128)S(1)}, f32[2,512]{1,0:T(2,128)}, u32[]{:S(2)}) copy-start(f32[2,512]{1,0:T(2,128)} %param.24) | copy-start | bytes 12292
  7.2 17.3 %copy-start.66 = (bf16[512,32]{0,1:T(8,128)(2,1)S(1)}, bf16[512,32]{0,1:T(8,128)(2,1)}, u32[]{:S(2)}) copy-start(bf16[512,32]{0,1:T(8,128)(2,1)} %param.16) | copy-start | bytes 98308
  8.0 10.2 %collective-permute-start = (bf16[4,1,128]{2,1,0:T(2,128)(2,1)S(1)}, bf16[4,1,128]{2,1,0:T(2,128)(2,1)S(1)}, u32[]{:S(2)}, u32[]{:S(2)}) collective-permute-start(bf16[4,1,128]{2,1,0:T(2,128)(2,1)S(1)} %get-tuple-element.110), channel_id=1, source_target_pairs={{0,16},{16,32},{32,48},{48,64},{64,80},{80,96},{96,112},{1,17},{17... | collective-permute-start | bytes 3080 | tf_op jit(solution)/shard_map/ppermute | solution.py:23
  12.4 5.9 collective-permute-start.1
  14.7 460.3 %copy-start.17 = (f32[1,128,512]{2,1,0:T(8,128)}, f32[1,128,512]{2,1,0:T(8,128)S(1)}, u32[]{:S(2)}) copy-start(f32[1,128,512]{2,1,0:T(8,128)S(1)} %get-tuple-element.149) | copy-start | bytes 786436
  14.8 16.0 %copy-start.77 = (f32[128]{0:T(128)}, f32[128]{0:T(128)S(1)}, u32[]{:S(2)}) copy-start(f32[128]{0:T(128)S(1)} %compare_select_fusion) | copy-start | bytes 1540
  18.5 7.3 collective-permute-start.2
  22.5 7.8 %collective-permute-start.3 = (bf16[4,258,1]{2,1,0:T(8,128)(2,1)S(1)}, bf16[4,258,1]{2,1,0:T(8,128)(2,1)S(1)}, u32[]{:S(2)}, u32[]{:S(2)}) collective-permute-start(bf16[4,258,1]{2,1,0:T(8,128)(2,1)S(1)} %get-tuple-element.109), channel_id=1, source_target_pairs={{1,0},{2,1},{3,2},{4,3},{5,4},{6,5},{7,6},{8,7},{9,8},{10,9},{11,1... | collective-permute-start | bytes 6200 | tf_op jit(solution)/shard_map/ppermute | solution.py:24
  391.4 10.7 %copy-start.25 = (f32[64,4,32,4]{0,1,2,3:T(4,128)S(1)}, f32[64,4,32,4]{0,1,2,3:T(4,128)}, u32[]{:S(2)}) copy-start(f32[64,4,32,4]{0,1,2,3:T(4,128)} %copy.258) | copy-start | bytes 393220
  391.4 10.8 %copy-start.26 = (f32[64,4,32,4]{0,1,2,3:T(4,128)S(1)}, f32[64,4,32,4]{0,1,2,3:T(4,128)}, u32[]{:S(2)}) copy-start(f32[64,4,32,4]{0,1,2,3:T(4,128)} %copy.259) | copy-start | bytes 393220
  391.4 10.8 %copy-start.27 = (f32[64,4,32,4]{0,1,2,3:T(4,128)S(1)}, f32[64,4,32,4]{0,1,2,3:T(4,128)}, u32[]{:S(2)}) copy-start(f32[64,4,32,4]{0,1,2,3:T(4,128)} %copy.260) | copy-start | bytes 393220
  391.4 10.8 %copy-start.28 = (f32[64,4,32,4]{0,1,2,3:T(4,128)S(1)}, f32[64,4,32,4]{0,1,2,3:T(4,128)}, u32[]{:S(2)}) copy-start(f32[64,4,32,4]{0,1,2,3:T(4,128)} %copy.261) | copy-start | bytes 393220
  391.4 10.8 %copy-start.29 = (f32[64,4,32,4]{0,1,2,3:T(4,128)S(1)}, f32[64,4,32,4]{0,1,2,3:T(4,128)}, u32[]{:S(2)}) copy-start(f32[64,4,32,4]{0,1,2,3:T(4,128)} %copy.262) | copy-start | bytes 393220
  391.4 10.8 %copy-start.30 = (f32[64,4,32,4]{0,1,2,3:T(4,128)S(1)}, f32[64,4,32,4]{0,1,2,3:T(4,128)}, u32[]{:S(2)}) copy-start(f32[64,4,32,4]{0,1,2,3:T(4,128)} %copy.263) | copy-start | bytes 393220
  391.4 10.8 %copy-start.31 = (f32[64,4,32,4]{0,1,2,3:T(4,128)S(1)}, f32[64,4,32,4]{0,1,2,3:T(4,128)}, u32[]{:S(2)}) copy-start(f32[64,4,32,4]{0,1,2,3:T(4,128)} %copy.264) | copy-start | bytes 393220
  391.4 10.8 %copy-start.32 = (f32[64,4,32,4]{0,1,2,3:T(4,128)S(1)}, f32[64,4,32,4]{0,1,2,3:T(4,128)}, u32[]{:S(2)}) copy-start(f32[64,4,32,4]{0,1,2,3:T(4,128)} %copy.265) | copy-start | bytes 393220
  391.4 10.8 %copy-start.33 = (f32[64,4,32,4]{0,1,2,3:T(4,128)S(1)}, f32[64,4,32,4]{0,1,2,3:T(4,128)}, u32[]{:S(2)}) copy-start(f32[64,4,32,4]{0,1,2,3:T(4,128)} %copy.266) | copy-start | bytes 393220
  391.4 10.8 %copy-start.79 = (f32[32]{0:T(128)S(1)}, f32[32]{0:T(128)}, u32[]{:S(2)}) copy-start(f32[32]{0:T(128)} %param.15) | copy-start | bytes 388
  426.7 19.9 %copy-start.76 = (f32[512]{0:T(512)S(1)}, f32[512]{0:T(512)}, u32[]{:S(2)}) copy-start(f32[512]{0:T(512)} %param.19) | copy-start | bytes 6148
  428.7 20.4 %all-to-all-start = ((bf16[64,32,128]{2,1,0:T(8,128)(2,1)}), bf16[64,32,128]{2,1,0:T(8,128)(2,1)S(1)}, u32[]{:S(2)}, u32[]{:S(2)}) async-start(bf16[64,32,128]{2,1,0:T(8,128)(2,1)} %copy.299), calls=%async_computation | async-start | bytes 1048576 | tf_op jit(solution)/shard_map/all_to_all | solution.py:187
  438.1 24.7 %copy-start.75 = (f32[512]{0:T(512)S(1)}, f32[512]{0:T(512)}, u32[]{:S(2)}) copy-start(f32[512]{0:T(512)} %param.18) | copy-start | bytes 6148
  449.9 33.1 %all-to-all-start.3 = ((bf16[4,2,128,512]{3,0,1,2:T(4,128)(2,1)}), bf16[4,2,128,512]{3,0,1,2:T(4,128)(2,1)S(1)}, u32[]{:S(2)}, u32[]{:S(2)}) async-start(bf16[4,2,128,512]{3,0,1,2:T(4,128)(2,1)} %copy.316), calls=%async_computation.3 | async-start | bytes 2097152 | tf_op jit(solution)/shard_map/all_to_all | solution.py:156
  479.2 17.1 %copy-start.63 = (bf16[128,512,1]{1,0,2:T(8,128)(2,1)S(1)}, bf16[128,512,1]{1,0,2:T(8,128)(2,1)}, u32[]{:S(2)}) copy-start(bf16[128,512,1]{1,0,2:T(8,128)(2,1)} %get-tuple-element.121) | copy-start | bytes 393220
  479.2 17.1 %copy-start.64 = (bf16[128,512,1]{1,0,2:T(8,128)(2,1)S(1)}, bf16[128,512,1]{1,0,2:T(8,128)(2,1)}, u32[]{:S(2)}) copy-start(bf16[128,512,1]{1,0,2:T(8,128)(2,1)} %get-tuple-element.122) | copy-start | bytes 393220
  484.0 29.0 %all-to-all-start.1 = ((bf16[4,2,128,512]{3,1,0,2:T(2,128)(2,1)}), bf16[4,2,128,512]{3,1,0,2:T(2,128)(2,1)}, u32[]{:S(2)}, u32[]{:S(2)}) async-start(bf16[4,2,128,512]{3,1,0,2:T(2,128)(2,1)} %copy.302), calls=%async_computation.1 | async-start | bytes 2097152 | tf_op jit(solution)/shard_map/all_to_all | solution.py:156
  494.2 8.2 %copy-start.6 = (f32[2,8,64,64]{3,2,1,0:T(8,128)S(1)}, f32[2,8,64,64]{3,2,1,0:T(8,128)}, u32[]{:S(2)}) copy-start(f32[2,8,64,64]{3,2,1,0:T(8,128)} %param.23) | copy-start | bytes 786436
  499.1 17.6 %copy-start.3 = (f32[2,8,64,64]{3,2,1,0:T(8,128)S(1)}, f32[2,8,64,64]{3,2,1,0:T(8,128)}, u32[]{:S(2)}) copy-start(f32[2,8,64,64]{3,2,1,0:T(8,128)} %param.21) | copy-start | bytes 786436
  501.0 18.3 %copy-start.13 = (f32[128,512]{0,1:T(8,128)}, f32[128,512]{0,1:T(8,128)S(1)}, u32[]{:S(2)}) copy-start(f32[128,512]{0,1:T(8,128)S(1)} %copy.319) | copy-start | bytes 786436
  519.4 8.5 %copy-start.4 = (f32[128,512]{0,1:T(8,128)}, f32[128,512]{0,1:T(8,128)S(1)}, u32[]{:S(2)}) copy-start(f32[128,512]{0,1:T(8,128)S(1)} %copy.306) | copy-start | bytes 786436
  519.4 10.8 %copy-start.22 = (f32[8,128,64]{1,2,0:T(8,128)S(1)}, f32[8,128,64]{1,2,0:T(8,128)}, u32[]{:S(2)}) copy-start(f32[8,128,64]{1,2,0:T(8,128)} %fusion.94) | copy-start | bytes 786436
  519.4 10.7 %copy-start.67 = (f32[8,64]{1,0:T(8,128)S(1)}, f32[8,64]{1,0:T(8,128)}, u32[]{:S(2)}) copy-start(f32[8,64]{1,0:T(8,128)} %add.394) | copy-start | bytes 6148
  519.5 12.3 %copy-start.7 = (f32[2,8,64,64]{3,2,1,0:T(8,128)S(1)}, f32[2,8,64,64]{3,2,1,0:T(8,128)}, u32[]{:S(2)}) copy-start(f32[2,8,64,64]{3,2,1,0:T(8,128)} %param.23) | copy-start | bytes 786436
  519.5 12.3 %copy-start.14 = (f32[128,512]{0,1:T(8,128)S(1)}, f32[128,512]{0,1:T(8,128)}, u32[]{:S(2)}) copy-start(f32[128,512]{0,1:T(8,128)} %copy-done.13) | copy-start | bytes 786436
  519.5 12.3 %copy-start.61 = (f32[8,128,64]{1,2,0:T(8,128)S(1)}, f32[8,128,64]{1,2,0:T(8,128)}, u32[]{:S(2)}) copy-start(f32[8,128,64]{1,2,0:T(8,128)} %fusion.85) | copy-start | bytes 786436
  545.3 12.1 %copy-start.15 = (f32[128,512]{0,1:T(8,128)S(1)}, f32[128,512]{0,1:T(8,128)}, u32[]{:S(2)}) copy-start(f32[128,512]{0,1:T(8,128)} %copy-done.13) | copy-start | bytes 786436
  545.3 14.3 %copy-start.8 = (f32[2,8,64,64]{3,2,1,0:T(8,128)S(1)}, f32[2,8,64,64]{3,2,1,0:T(8,128)}, u32[]{:S(2)}) copy-start(f32[2,8,64,64]{3,2,1,0:T(8,128)} %param.23) | copy-start | bytes 786436
  549.1 24.7 %all-to-all-start.4 = ((bf16[512,2,1,512]{3,1,2,0:T(2,128)(2,1)}), bf16[512,2,1,512]{3,1,2,0:T(2,128)(2,1)}, u32[]{:S(2)}, u32[]{:S(2)}) async-start(bf16[512,2,1,512]{3,1,2,0:T(2,128)(2,1)} %copy.331), calls=%async_computation.4 | async-start | bytes 2097152 | tf_op jit(solution)/shard_map/all_to_all | solution.py:160
  561.2 8.5 %copy-start.12 = (f32[128,8,64]{0,2,1:T(8,128)S(1)}, f32[128,8,64]{0,2,1:T(8,128)}, u32[]{:S(2)}) copy-start(f32[128,8,64]{0,2,1:T(8,128)} %get-tuple-element.130) | copy-start | bytes 786436
  562.8 7.4 copy-start.5
  562.8 7.4 copy-start.11
  568.8 14.3 %copy-start.18 = (f32[1,128,512]{2,1,0:T(8,128)S(1)}, f32[1,128,512]{2,1,0:T(8,128)}, u32[]{:S(2)}) copy-start(f32[1,128,512]{2,1,0:T(8,128)} %copy-done.17) | copy-start | bytes 786436
  573.8 28.0 %all-to-all-start.2 = ((bf16[512,2,1,512]{3,1,2,0:T(2,128)(2,1)}), bf16[512,2,1,512]{3,1,2,0:T(2,128)(2,1)}, u32[]{:S(2)}, u32[]{:S(2)}) async-start(bf16[512,2,1,512]{3,1,2,0:T(2,128)(2,1)} %copy.312), calls=%async_computation.2 | async-start | bytes 2097152 | tf_op jit(solution)/shard_map/all_to_all | solution.py:160
  583.0 167.5 %all-reduce.4.cloned.1.call-start = ((), (), s32[]{:S(2)}) async-start(), calls=%async_computation.5 | async-start | bytes 2621440 | tf_op jit(solution)/shard_map/psum | solution.py:258
  594.6 9.7 %copy-start.78 = (f32[128]{0:T(128)S(1)}, f32[128]{0:T(128)}, u32[]{:S(2)}) copy-start(f32[128]{0:T(128)} %copy-done.77) | copy-start | bytes 1540
  (42 other events, 219.5 us)
Sparse Core Ops, SparseCore 0:
  604.5 146.0 all-reduce.3
where the time goes:
time: 768 us; the launch traced here: 763 us
  local copies, waits for them, and re-layouts  425 us (55%)
  waiting for transfers between devices  93.2 us (12%)
  matrix products  87.2 us (11%)
  blocking collectives  64.3 us (8%)
  starting transfers between devices  57.4 us (7%)
  other arithmetic  20.4 us (3%)
  between operations  15.7 us (2%)
    mul x73, local copies, waits for them, and re-layouts, conv_project(): enc_taps[tap_index][:, None, None]  370 us
    psum x1, waiting for transfers between devices, body(): lax.psum((grad_w_in, grad_b_in, grad_ln_gain, grad_ln_bias, grad_w1, grad...  73.8 us
    psum x1, blocking collectives, body(): lax.psum((grad_w_in, grad_b_in, grad_ln_gain, grad_ln_bias, grad_w1, grad...  64.3 us
    dot_general x4, matrix products, conv_project(): jnp.einsum('caybx,cyxo->abo', blocks, patch_proj, preferred_element_type=...  23.6 us
    all_to_all x2, starting transfers between devices, toward_modes(): lax.all_to_all(values, ('rows', 'cols'), split_axis=2, concat_axis=0, til...  21.2 us
  transfers between devices with their start and end apart: 10, of which 6 were waited for; matrix products, arithmetic and copies ran while one was open for 11% of the time, Pallas kernels for 0%

commit v1 on v0

v1 whole, which is shorter than its diff:
```python
import functools
import math

import jax
import jax.numpy as jnp
import ml_dtypes
import numpy as np
from jax import lax
from jax.experimental import pallas as pl
from jax.experimental.pallas import tpu as pltpu
from jax.sharding import PartitionSpec as P

F32 = jnp.float32
BF16 = jnp.bfloat16
MESH = pl.DeviceIdType.MESH
HIGHEST = lax.Precision.HIGHEST

NR, NC = 8, 16
ND = NR * NC
LAT = 512
WIDTH = 512
KH = 128
ROWS = 4
FRAMES = 4
STEP = 37
EPS = 1e-05
FACTOR = LAT ** (-0.5)
CUBE = 0.044715
ROOT = math.sqrt(2.0 / math.pi)


def tables():
    n = np.arange(LAT)
    k = np.arange(ND)
    angle = ((k[:, None] * n[None, :]) % LAT).astype(np.float32) * np.float32(2.0 * math.pi / LAT)
    fwd = np.stack([np.cos(angle.astype(np.float64)), -np.sin(angle.astype(np.float64))]).astype(np.float32)
    inv = fwd * np.where(k == 0, 1.0, 2.0).astype(np.float32)[None, :, None]
    order = lambda t: t.reshape(2, 32, 4, LAT).transpose(2, 0, 1, 3).reshape(256, LAT).astype(ml_dtypes.bfloat16)
    m = np.arange(KH) - KH // 2
    u = (np.mod(m[:, None] * n[None, :], LAT)).astype(np.float32) * np.float32(2.0 * math.pi / LAT)
    cos, sin = np.cos(u.astype(np.float64)), np.sin(u.astype(np.float64))
    rot = np.concatenate([np.stack([cos, sin], -1), np.stack([-sin, cos], -1)], 0)
    rot = rot.astype(np.float32).reshape(2 * KH, 2 * LAT).astype(ml_dtypes.bfloat16)
    wf, wi = order(fwd), order(inv)
    place = np.zeros((16, 48, 144), np.float32)
    for y in range(4):
        for x in range(4):
            for part in range(3):
                for tap in range(9):
                    place[4 * y + x, 16 * part + tap, 48 * part + 8 * (y + tap // 3) + x + tap % 3] = 1.0
                place[4 * y + x, 16 * part + 9, 48 * part + 6] = 1.0
    return wf, wi, np.ascontiguousarray(wf.T), np.ascontiguousarray(wi.T), rot, np.ascontiguousarray(rot.T), place.astype(ml_dtypes.bfloat16)


def dot(a, b, precision=None):
    return jnp.dot(a, b, preferred_element_type=F32, precision=precision)


def dot_t(a, b, dims, precision=None):
    return lax.dot_general(a, b, (dims, ((), ())), preferred_element_type=F32, precision=precision)


def gelu_pair(v):
    squared = v * v
    t = jnp.tanh(ROOT * (v + CUBE * (squared * v)))
    half = 0.5 * (1.0 + t)
    slope = half + 0.5 * v * (1.0 - t * t) * (ROOT * (1.0 + (3.0 * CUBE) * squared))
    return v * half, slope


def kernel(
    frames, taps, bias, proj, w_in, b_in, gain, lbias, w1, b1, w2, b2, cot_hbm,
    wf, wi, wft, wit, rot, rott, place,
    den_hbm, gwin, gbin, ggain, gbias, gw1, gb1, gw2, gb2,
    cot, ft, fsend, htop, hbot, frecv, rtop, rbot, est, wbig, projt, tp, lat, emb, nrm, istd, den,
    stage, snd, rcv, wc1, wc2, bc, wsend, wrecv, agw, fsnd, frcv, agf,
    lsem, fss, frs, hss, hrs, ass, ars, als, wss, wrs, gss, grs, rss, rrs, qss, qrs,
):
    r = lax.axis_index("rows")
    c = lax.axis_index("cols")
    me = r * NC + c
    kg = me // 4
    cg = lax.rem(me, 4)

    def coord(d):
        return (d // NC, lax.rem(d, NC))

    def peer(i):
        return lax.rem(me + lax.rem(i * STEP, ND), ND)

    cot_in = pltpu.make_async_copy(cot_hbm, cot, lsem.at[0])
    cot_in.start()
    barrier = pltpu.get_barrier_semaphore()

    @pl.loop(1, ND)
    def _(i):
        pl.semaphore_signal(barrier, inc=1, device_id=coord(peer(i)), device_id_type=MESH)

    zero8 = jnp.zeros((8, 128), F32)
    for f in range(FRAMES):
        ft[f, 0:8, :] = zero8
        ft[f, 264:272, :] = zero8
        ft[f, 8:264, :] = frames[f].astype(F32)
    for f in range(FRAMES):
        for j in range(NC):
            fsend[j, f] = ft[f, 16 * j + 7 : 16 * j + 31, :].reshape(3, 8, 128).astype(BF16)
        htop[f] = ft[f, 263:271, :].astype(BF16)
        hbot[f] = ft[f, 7:15, :].astype(BF16)
    pl.semaphore_wait(barrier, ND - 1)

    def frame_copy(i):
        j = lax.rem(c + i, NC)
        return pltpu.make_async_remote_copy(
            fsend.at[j], frecv.at[c], fss, frs, device_id=(r, j), device_id_type=MESH)

    @pl.loop(1, NC)
    def _(i):
        frame_copy(i).start()

    own_frames = pltpu.make_async_copy(fsend.at[c], frecv.at[c], lsem.at[1])
    own_frames.start()

    @pl.when(r < NR - 1)
    def _():
        pltpu.make_async_remote_copy(
            htop, rtop.at[c], hss.at[0], hrs.at[0], device_id=(r + 1, 0), device_id_type=MESH).start()

    @pl.when(r > 0)
    def _():
        pltpu.make_async_remote_copy(
            hbot, rbot.at[c], hss.at[1], hrs.at[1], device_id=(r - 1, NC - 1), device_id_type=MESH).start()

    has_top = jnp.logical_and(c == 0, r > 0)
    has_bot = jnp.logical_and(c == NC - 1, r < NR - 1)

    @pl.when(jnp.logical_not(has_top))
    def _():
        rtop[...] = jnp.zeros(rtop.shape, BF16)

    @pl.when(jnp.logical_not(has_bot))
    def _():
        rbot[...] = jnp.zeros(rbot.shape, BF16)

    def send_all(e):
        pltpu.make_async_copy(snd.at[e, me], rcv.at[e, me], als.at[e]).start()

        @pl.loop(1, ND)
        def _(i):
            d = peer(i)
            pltpu.make_async_remote_copy(
                snd.at[e, d], rcv.at[e, me], ass.at[e], ars.at[e], device_id=coord(d), device_id_type=MESH).start()

    def all_but_one(buf, ss, rs, count):
        part = buf.at[pl.ds(0, count)]
        return pltpu.make_async_remote_copy(part, part, ss, rs, device_id=coord(peer(1)), device_id_type=MESH)

    def recv_all(e):
        pltpu.make_async_copy(snd.at[e, me], rcv.at[e, me], als.at[e]).wait()
        all_but_one(rcv.at[e], ass.at[e], ars.at[e], ND - 1).wait_recv()

    def put_rows(h, value):
        for k4 in range(4):
            for p in range(2):
                rows = value[k4 * 64 + p * 32 : k4 * 64 + p * 32 + 32, :]
                for g in range(4):
                    stage[k4, pl.ds(8 * g + 2 * h + p, 32, stride=32), :] = rows[:, 128 * g : 128 * g + 128]

    def pack(e):
        for k4 in range(4):
            snd[e, :, :, 128 * k4 : 128 * k4 + 128] = stage[k4].reshape(ND, 8, 128).astype(BF16)

    cot_in.wait()
    for h in range(ROWS):
        put_rows(h, dot(wi[...], cot[h]) * FACTOR)
    pack(0)
    send_all(0)

    tp[...] = jnp.zeros(tp.shape, F32)
    tp[0:9, :] = taps[...]
    tp[9:10, :] = bias[...]
    whole = tp[...]
    high = whole.astype(BF16)
    rest = whole - high.astype(F32)
    mid = rest.astype(BF16)
    low = (rest - mid.astype(F32)).astype(BF16)
    parts = jnp.concatenate([high, mid, low], axis=0)
    for yx in range(16):
        wbig[32 * yx : 32 * yx + 32, :] = dot_t(parts, place[yx], ((0,), (0,))).astype(BF16)
    row = lax.broadcasted_iota(jnp.int32, (512, 512), 0)
    col = lax.broadcasted_iota(jnp.int32, (512, 512), 1)
    to_yxc = (row == (col & 31) * 16 + (col >> 5)).astype(F32).astype(BF16)
    projt[...] = dot_t(proj[...], to_yxc, ((0,), (0,))).astype(BF16)
    to_phase = (row == (col & 127) * 4 + (col >> 7)).astype(F32).astype(BF16)
    for wc, w in ((wc1, w1), (wc2, w2)):
        wc[...] = jnp.zeros(wc.shape, F32)
        for b in range(2):
            real = w[0, 2 * cg + b]
            imag = w[1, 2 * cg + b]
            lo, hi = 64 * b, 64 * b + 64
            wc[lo:hi, lo:hi] = real
            wc[128 + lo : 128 + hi, 128 + lo : 128 + hi] = real
            wc[lo:hi, 128 + lo : 128 + hi] = imag
            wc[128 + lo : 128 + hi, lo:hi] = -imag
    lanes = pl.ds(pl.multiple_of(cg * 128, 128), 128)
    bias1 = jnp.concatenate([b1[0:1, lanes], b1[1:2, lanes]], axis=1)
    bias2 = jnp.concatenate([b2[0:1, lanes], b2[1:2, lanes]], axis=1)
    for f in range(FRAMES):
        for t in range(4):
            est[f, t, pl.ds(6, 24, stride=8), :] = jnp.ones((24, 128), F32)
            est[f, t, pl.ds(7, 24, stride=8), :] = jnp.zeros((24, 128), F32)

    own_frames.wait()
    all_but_one(frecv, fss, frs, NC - 1).wait_recv()

    @pl.when(has_top)
    def _():
        pltpu.make_async_remote_copy(rtop, rtop, hss.at[0], hrs.at[0], device_id=(r, c), device_id_type=MESH).wait_recv()

    @pl.when(has_bot)
    def _():
        pltpu.make_async_remote_copy(rbot, rbot, hss.at[1], hrs.at[1], device_id=(r, c), device_id_type=MESH).wait_recv()

    split = []
    for g in range(4):
        pieces = []
        for j in range(4):
            v = frecv[4 * g + j].astype(F32)
            up = v[:, 0] + rtop[4 * g + j].astype(F32)
            down = v[:, 2] + rbot[4 * g + j].astype(F32)
            pieces.append(jnp.stack([up, v[:, 1], down], axis=1).reshape(96, 128).astype(BF16))
        split.append(dot(jnp.concatenate(pieces, axis=1), to_phase))
    lane = lax.broadcasted_iota(jnp.int32, (96, 512), 1)
    first = jnp.concatenate([s[:, 0:128] for s in split], axis=1)
    last = jnp.concatenate([s[:, 384:512] for s in split], axis=1)
    before = jnp.where(lane == 0, 0.0, pltpu.roll(last, 1, axis=1))
    after = jnp.where(lane == LAT - 1, 0.0, pltpu.roll(first, LAT - 1, axis=1))
    for t in range(4):
        own = slice(128 * t, 128 * t + 128)
        planes = [before[:, own]] + [split[t][:, 128 * q : 128 * q + 128] for q in range(4)] + [after[:, own]]
        for x, plane in enumerate(planes):
            for f in range(FRAMES):
                est[f, t, pl.ds(x, 24, stride=8), :] = plane[24 * f : 24 * f + 24, :]

    @pl.loop(0, ROWS)
    def _(h):
        for f in range(FRAMES):
            top = pl.multiple_of(32 * h, 32)
            patch = jnp.concatenate([est[f, t, pl.ds(top, 48), :] for t in range(4)], axis=1).astype(BF16)
            hidden = dot(wbig[...], jnp.concatenate([patch, patch, patch], axis=0))
            hidden = jnp.maximum(hidden, 0.0).astype(BF16)
            lat[h, 32 * f : 32 * f + 32, :] = dot(projt[...], hidden).astype(BF16)

    for h in range(ROWS):
        embedded = dot_t(lat[h], w_in[...], ((0,), (0,))) + b_in[...]
        emb[h] = embedded
        centered = embedded - jnp.mean(embedded, axis=1, keepdims=True)
        inverse = lax.rsqrt(jnp.mean(centered * centered, axis=1, keepdims=True) + EPS)
        normalized = centered * inverse
        istd[h] = inverse
        nrm[h] = normalized
        normed = (normalized * gain[...] + lbias[...]).astype(BF16)
        put_rows(h, dot(wf[...], normed) * FACTOR)
    pack(1)
    send_all(1)

    def to_modes(e):
        x = rcv[e].astype(F32).reshape(2 * LAT, 512).astype(BF16)
        return stacked(dot(rot[...], x) * FACTOR)

    def stacked(v):
        return jnp.concatenate(
            [jnp.concatenate([v[0:KH, 128 * q : 128 * q + 128], v[KH:, 128 * q : 128 * q + 128]], axis=1) for q in range(4)], axis=0)

    def unstacked(v):
        return jnp.concatenate(
            [jnp.concatenate([v[KH * q : KH * q + KH, 128 * p : 128 * p + 128] for q in range(4)], axis=1) for p in range(2)], axis=0)

    def from_modes(e, v):
        back = dot(rott[...], unstacked(v).astype(BF16)) * FACTOR
        snd[e] = back.reshape(ND, 8, 512).astype(BF16)
        send_all(e)

    recv_all(0)
    grad = to_modes(0)
    recv_all(1)
    coeffs = to_modes(1)
    pre = dot(coeffs, wc1[...], HIGHEST) + bias1
    act, slope = gelu_pair(pre)
    from_modes(2, dot(act, wc2[...], HIGHEST) + bias2)
    back = dot_t(grad, wc2[...], ((1,), (1,)), HIGHEST) * slope
    from_modes(3, dot_t(back, wc1[...], ((1,), (1,)), HIGHEST))

    half = lax.broadcasted_iota(jnp.int32, (64, 128), 1) < 64

    def weight_grad(left, right):
        g = dot_t(left, right, ((0,), (0,)), HIGHEST)
        real = g[0:128, 0:128] + g[128:256, 128:256]
        imag = g[0:128, 128:256] - g[128:256, 0:128]
        return [jnp.where(half, v[0:64, :], v[64:128, :]) for v in (real, imag)]

    tiles = weight_grad(coeffs, back) + weight_grad(act, grad)
    wsend[...] = jnp.concatenate(tiles, axis=0).reshape(32, 8, 128)
    wrecv[kg] = wsend[kg]

    @pl.loop(1, 32)
    def _(i):
        j = lax.rem(kg + i, 32)
        pltpu.make_async_remote_copy(
            wsend.at[j], wrecv.at[kg], wss, wrs, device_id=coord(4 * j + cg), device_id_type=MESH).start()

    sum1 = jnp.sum(back, axis=0, keepdims=True)
    sum2 = jnp.sum(grad, axis=0, keepdims=True)
    bc[...] = jnp.zeros(bc.shape, F32)
    for p in range(2):
        bc[p : p + 1, lanes] = sum1[:, 128 * p : 128 * p + 128]
        bc[2 + p : 3 + p, lanes] = sum2[:, 128 * p : 128 * p + 128]

    def get_rows(e, h):
        blocks = []
        for k4 in range(4):
            for q in range(2):
                blocks.append(jnp.concatenate(
                    [stage[k4, pl.ds(8 * g + 2 * h + q, 32, stride=32), :] for g in range(4)], axis=1))
        return jnp.concatenate(blocks, axis=0).astype(BF16)

    def unpack(e):
        for k4 in range(4):
            stage[k4] = rcv[e, :, :, 128 * k4 : 128 * k4 + 128].astype(F32).reshape(8 * ND, 128)

    recv_all(2)
    unpack(2)
    for h in range(ROWS):
        den[h] = (emb[h] + dot(wit[...], get_rows(2, h)) * FACTOR).astype(BF16)
        pltpu.make_async_copy(den.at[h], den_hbm.at[h], lsem.at[2 + h]).start()

    all_but_one(wrecv, wss, wrs, 31).wait_recv()
    total = wrecv[0]
    for j in range(1, 32):
        total = total + wrecv[j]
    agw[kg, cg] = total

    @pl.loop(1, ND)
    def _(i):
        pltpu.make_async_remote_copy(
            agw.at[kg, cg], agw.at[kg, cg], gss, grs, device_id=coord(peer(i)), device_id_type=MESH).start()

    recv_all(3)
    unpack(3)
    sums = [jnp.zeros((1, WIDTH), F32) for _ in range(3)]
    weight = jnp.zeros((128, WIDTH), F32)
    for h in range(ROWS):
        gn = dot(wft[...], get_rows(3, h)) * FACTOR
        normalized = nrm[h]
        sums[1] = sums[1] + jnp.sum(gn * normalized, axis=0, keepdims=True)
        sums[2] = sums[2] + jnp.sum(gn, axis=0, keepdims=True)
        scaled = gn * gain[...]
        ge = cot[h].astype(F32) + istd[h] * (
            scaled
            - jnp.mean(scaled, axis=1, keepdims=True)
            - normalized * jnp.mean(scaled * normalized, axis=1, keepdims=True))
        sums[0] = sums[0] + jnp.sum(ge, axis=0, keepdims=True)
        weight = weight + dot(lat[h], ge.astype(BF16))

    for b in range(4):
        own = slice(128 * b, 128 * b + 128)
        for a in range(32):
            fsnd[4 * a + b, 0:4, :] = weight[4 * a : 4 * a + 4, own]
        for a in range(3):
            fsnd[4 * a + b, 4:5, :] = sums[a][:, own]
        for a in range(4):
            fsnd[4 * (a + 3) + b, 4:5, :] = bc[a : a + 1, own]
        for a in range(7, 32):
            fsnd[4 * a + b, 4:5, :] = jnp.zeros((1, 128), F32)
    for d in range(ND):
        fsnd[d, 5:8, :] = jnp.zeros((3, 128), F32)
    frcv[me] = fsnd[me]

    @pl.loop(1, ND)
    def _(i):
        d = peer(i)
        pltpu.make_async_remote_copy(
            fsnd.at[d], frcv.at[me], rss, rrs, device_id=coord(d), device_id_type=MESH).start()

    all_but_one(frcv, rss, rrs, ND - 1).wait_recv()
    agf[me] = jnp.sum(frcv[...], axis=0)

    @pl.loop(1, ND)
    def _(i):
        pltpu.make_async_remote_copy(
            agf.at[me], agf.at[me], qss, qrs, device_id=coord(peer(i)), device_id_type=MESH).start()

    everyone = dict(device_id=coord(peer(1)), device_id_type=MESH)
    agw_most = pltpu.make_async_remote_copy(frcv.at[pl.ds(0, ND - 1)], frcv.at[pl.ds(0, ND - 1)], gss, grs, **everyone)
    agw_most.wait_recv()
    for w, (gw, gb) in enumerate(((gw1, gb1), (gw2, gb2))):
        for p in range(2):
            for g in range(4):
                v = agw[16 * w + 8 * p : 16 * w + 8 * p + 8, g].reshape(64, 128)
                gw[p, 2 * g] = v[:, 0:64]
                gw[p, 2 * g + 1] = v[:, 64:128]

    all_but_one(agf, qss, qrs, ND - 1).wait_recv()
    small = [gbin, ggain, gbias]
    for b in range(4):
        own = slice(128 * b, 128 * b + 128)
        for a in range(32):
            gwin[4 * a : 4 * a + 4, own] = agf[4 * a + b, 0:4, :]
        for a in range(3):
            small[a][:, own] = agf[4 * a + b, 4:5, :]
        for a in range(2):
            gb1[a : a + 1, own] = agf[4 * (a + 3) + b, 4:5, :]
            gb2[a : a + 1, own] = agf[4 * (a + 5) + b, 4:5, :]

    for h in range(ROWS):
        pltpu.make_async_copy(den.at[h], den_hbm.at[h], lsem.at[2 + h]).wait()
    all_but_one(frecv, fss, frs, NC - 1).wait_send()

    @pl.when(r < NR - 1)
    def _():
        pltpu.make_async_remote_copy(htop, htop, hss.at[0], hrs.at[0], device_id=(r, c), device_id_type=MESH).wait_send()

    @pl.when(r > 0)
    def _():
        pltpu.make_async_remote_copy(hbot, hbot, hss.at[1], hrs.at[1], device_id=(r, c), device_id_type=MESH).wait_send()

    for e in range(4):
        all_but_one(rcv.at[e], ass.at[e], ars.at[e], ND - 1).wait_send()
    all_but_one(wrecv, wss, wrs, 31).wait_send()
    agw_most.wait_send()
    all_but_one(frcv, rss, rrs, ND - 1).wait_send()
    all_but_one(agf, qss, qrs, ND - 1).wait_send()


def body(frames, enc_taps, enc_bias, enc_proj, w_in, b_in, ln_gain, ln_bias, spec_w1, spec_b1, spec_w2, spec_b2, cotangent):
    wf, wi, wft, wit, rot, rott, place = (jnp.asarray(t) for t in tables())
    vmem = pl.BlockSpec(memory_space=pltpu.VMEM)
    hbm = pl.BlockSpec(memory_space=pl.ANY)
    shape = jax.ShapeDtypeStruct
    dma = pltpu.SemaphoreType.DMA
    outs = pl.pallas_call(
        kernel,
        out_shape=(
            shape((ROWS, LAT, WIDTH), BF16), shape((128, WIDTH), F32), shape((1, WIDTH), F32), shape((1, WIDTH), F32),
            shape((1, WIDTH), F32), shape((2, 8, 64, 64), F32), shape((2, WIDTH), F32), shape((2, 8, 64, 64), F32),
            shape((2, WIDTH), F32)),
        in_specs=[vmem] * 12 + [hbm] + [vmem] * 7,
        out_specs=(hbm,) + (vmem,) * 8,
        scratch_shapes=[
            pltpu.VMEM((ROWS, LAT, WIDTH), BF16),
            pltpu.VMEM((FRAMES, 272, 128), F32),
            pltpu.VMEM((NC, FRAMES, 3, 8, 128), BF16),
            pltpu.VMEM((FRAMES, 8, 128), BF16),
            pltpu.VMEM((FRAMES, 8, 128), BF16),
            pltpu.VMEM((NC, FRAMES, 3, 8, 128), BF16),
            pltpu.VMEM((NC, FRAMES, 8, 128), BF16),
            pltpu.VMEM((NC, FRAMES, 8, 128), BF16),
            pltpu.VMEM((FRAMES, 4, 192, 128), F32),
            pltpu.VMEM((512, 144), BF16),
            pltpu.VMEM((32, 512), BF16),
            pltpu.VMEM((16, 32), F32),
            pltpu.VMEM((ROWS, 128, LAT), BF16),
            pltpu.VMEM((ROWS, LAT, WIDTH), F32),
            pltpu.VMEM((ROWS, LAT, WIDTH), F32),
            pltpu.VMEM((ROWS, LAT, 1), F32),
            pltpu.VMEM((ROWS, LAT, WIDTH), BF16),
            pltpu.VMEM((4, 8 * ND, 128), F32),
            pltpu.VMEM((4, ND, 8, 512), BF16),
            pltpu.VMEM((4, ND, 8, 512), BF16),
            pltpu.VMEM((256, 256), F32),
            pltpu.VMEM((256, 256), F32),
            pltpu.VMEM((8, WIDTH), F32),
            pltpu.VMEM((32, 8, 128), F32),
            pltpu.VMEM((32, 8, 128), F32),
            pltpu.VMEM((32, 4, 8, 128), F32),
            pltpu.VMEM((ND, 8, 128), F32),
            pltpu.VMEM((ND, 8, 128), F32),
            pltpu.VMEM((ND, 8, 128), F32),
            dma((8,)), dma(()), dma(()), dma((2,)), dma((2,)), dma((4,)), dma((4,)), dma((4,)),
            dma(()), dma(()), dma(()), dma(()), dma(()), dma(()), dma(()), dma(()),
        ],
        compiler_params=pltpu.CompilerParams(
            collective_id=0, has_side_effects=True, vmem_limit_bytes=64 * 1000 * 1000),
        name="step",
    )(
        frames, enc_taps, enc_bias.reshape(1, -1), enc_proj, w_in, b_in.reshape(1, -1), ln_gain.reshape(1, -1),
        ln_bias.reshape(1, -1), spec_w1, spec_b1, spec_w2, spec_b2, cotangent,
        wf, wi, wft, wit, rot, rott, place)
    den, gwin, gbin, ggain, gbias, gw1, gb1, gw2, gb2 = outs
    return (den, gwin, gbin.reshape(-1), ggain.reshape(-1), gbias.reshape(-1), gw1, gb1, gw2, gb2)


def solution(mesh):
    return jax.shard_map(
        body,
        mesh=mesh,
        in_specs=(P(None, "rows", "cols"),) + (P(),) * 11 + (P(("rows", "cols"), None, None),),
        out_specs=(P(("rows", "cols"), None, None),) + (P(),) * 8,
        check_vma=False,
    )
```

time: 768 us -> 121 us (0.16)
  local copies, waits for them, and re-layouts: 425 us -> 9.9 us
  Pallas kernels: 0 us -> 110 us
  waiting for transfers between devices: 93.2 us -> 0 us
  matrix products: 87.2 us -> 0 us
  blocking collectives: 64.3 us -> 0 us
  starting transfers between devices: 57.4 us -> 0 us
  other arithmetic: 20.4 us -> 0 us
  between operations: 15.7 us -> 0.71 us
    mul x73 -> x0, local copies, waits for them, and re-layouts: 370 us -> none  [conv_project(): enc_taps[tap_index][:, None, None]]
    pallas_call x0 -> x1, Pallas kernels: none -> 110 us  [body(): pl.pallas_call(kernel, out_shape=(shape((ROWS, LAT, WIDTH), BF16), shape(...]
    dot_general x38 -> x0, matrix products: 87.2 us -> none  [the longest x4 23.6 us: conv_project(): jnp.einsum('caybx,cyxo->abo', blocks, patch_proj, preferred_element_type=...]
    psum x1 -> x0, waiting for transfers between devices: 73.8 us -> none  [body(): lax.psum((grad_w_in, grad_b_in, grad_ln_gain, grad_ln_bias, grad_w1, grad...]
    psum x1 -> x0, blocking collectives: 64.3 us -> none  [body(): lax.psum((grad_w_in, grad_b_in, grad_ln_gain, grad_ln_bias, grad_w1, grad...]
    all_to_all x5 -> x0, starting transfers between devices: 45.8 us -> none  [the longest x2 21.2 us: toward_modes(): lax.all_to_all(values, ('rows', 'cols'), split_axis=2, concat_axis=0, til...]
    all_to_all x5 -> x0, waiting for transfers between devices: 14.5 us -> none  [the longest x2 7.47 us: toward_modes(): lax.all_to_all(values, ('rows', 'cols'), split_axis=2, concat_axis=0, til...]
    convert_element_type x5 -> x0, local copies, waits for them, and re-layouts: 13.7 us -> none  [the longest x1 3.75 us: body(): spectrum = (jnp.einsum('pkn,hnc->hpkc', wave_fwd, normed, preferred_eleme...]
  transfers between devices with their start and end apart: 10 -> 0, of which waited for: 6 -> 0; matrix products, arithmetic and copies ran while one was open for 11% -> 0% of each run, Pallas kernels for 0% -> 0%
where the time goes in v1:
time: 121 us
  Pallas kernels  110 us (91%)
  local copies, waits for them, and re-layouts  9.9 us (8%)
    pallas_call x1, Pallas kernels, body(): pl.pallas_call(kernel, out_shape=(shape((ROWS, LAT, WIDTH), BF16), shape(...  110 us
    unnamed x26, local copies, waits for them, and re-layouts  9.9 us

profile of v1, /device:TPU:1, one launch (start us, length us, event | category | flops | bytes accessed | tf_op | source)
XLA Modules:
  0.0 120.7 jit_solution(8384186446843538838)
XLA Ops:
  0.6 1.5 %copy.29.proj = bf16[512,32]{1,0:T(8,128)(2,1)} copy(bf16[512,32]{0,1:T(8,128)(2,1)} %param.23) | data formatting | bytes 65536 | tf_op args[3]
  2.2 110.1 %step.1 = (bf16[4,512,512]{2,1,0:T(8,128)(2,1)}, f32[128,512]{1,0:T(8,128)}, f32[1,512]{1,0:T(1,128)}, f32[1,512]{1,0:T(1,128)}, f32[1,512]{1,0:T(1,128)}, /*ind...) custom-call(bf16[4,256,128]{2,1,0:T(8,128)(2,1)} %frames.1, ...), custom_call_target="tpu_custom_call" | custom-call | tf_op jit(solution)/shard_map/step/pallas_call | solution.py:440
  112.3 0.0 copy-start.2
  112.3 0.0 copy-start.7
  112.3 0.0 copy-start.6
  112.3 0.0 copy-start.5
  112.3 0.0 copy-start.1
  112.3 0.0 copy-start.4
  112.3 0.0 copy-start
  112.3 3.1 %copy.39 = bf16[4,512,512]{2,1,0:T(8,128)(2,1)} copy(bf16[4,512,512]{2,1,0:T(8,128)(2,1)} %get-tuple-element.36) | data formatting | bytes 4194304
  115.5 0.0 copy-done.2
  115.5 0.0 copy-start.3
  115.5 0.7 copy.40
  116.2 0.0 copy-done.7
  116.2 0.6 copy.41
  116.8 0.0 copy-done.6
  116.8 0.6 copy.42
  117.4 0.0 copy-done.5
  117.4 0.6 copy.43
  117.9 0.0 copy-done.1
  117.9 0.8 copy.44
  118.7 0.0 copy-done.4
  118.7 0.6 copy.45
  119.3 0.0 copy-done
  119.3 0.8 copy.46
  120.1 0.0 copy-done.3
  120.1 0.6 copy.47
Async XLA Ops:
  112.3 3.2 %copy-start.2 = (f32[128,512]{1,0:T(8,128)S(1)}, f32[128,512]{1,0:T(8,128)}, u32[]{:S(2)}) copy-start(f32[128,512]{1,0:T(8,128)} %get-tuple-element.37) | copy-start | bytes 786436
  112.3 3.9 %copy-start.7 = (f32[1,512]{1,0:T(1,128)S(1)}, f32[1,512]{1,0:T(1,128)}, u32[]{:S(2)}) copy-start(f32[1,512]{1,0:T(1,128)} %get-tuple-element.20) | copy-start | bytes 6148
  112.3 4.5 %copy-start.6 = (f32[1,512]{1,0:T(1,128)S(1)}, f32[1,512]{1,0:T(1,128)}, u32[]{:S(2)}) copy-start(f32[1,512]{1,0:T(1,128)} %get-tuple-element.21) | copy-start | bytes 6148
  112.3 5.1 %copy-start.5 = (f32[1,512]{1,0:T(1,128)S(1)}, f32[1,512]{1,0:T(1,128)}, u32[]{:S(2)}) copy-start(f32[1,512]{1,0:T(1,128)} %get-tuple-element.22) | copy-start | bytes 6148
  112.3 5.6 %copy-start.1 = (f32[2,8,64,64]{3,2,1,0:T(8,128)S(1)}, f32[2,8,64,64]{3,2,1,0:T(8,128)}, u32[]{:S(2)}) copy-start(f32[2,8,64,64]{3,2,1,0:T(8,128)} %get-tuple-element.41) | copy-start | bytes 786436
  112.3 6.4 %copy-start.4 = (f32[2,512]{1,0:T(2,128)S(1)}, f32[2,512]{1,0:T(2,128)}, u32[]{:S(2)}) copy-start(f32[2,512]{1,0:T(2,128)} %get-tuple-element.42) | copy-start | bytes 12292
  112.3 7.0 %copy-start = (f32[2,8,64,64]{3,2,1,0:T(8,128)S(1)}, f32[2,8,64,64]{3,2,1,0:T(8,128)}, u32[]{:S(2)}) copy-start(f32[2,8,64,64]{3,2,1,0:T(8,128)} %get-tuple-element.43) | copy-start | bytes 786436
  115.5 4.6 %copy-start.3 = (f32[2,512]{1,0:T(2,128)S(1)}, f32[2,512]{1,0:T(2,128)}, u32[]{:S(2)}) copy-start(f32[2,512]{1,0:T(2,128)} %get-tuple-element.44) | copy-start | bytes 12292

commit v2 on v1

v2 whole, which is shorter than its diff:
```python
import itertools
import math
import random

import jax
import jax.numpy as jnp
import ml_dtypes
import numpy as np
from jax import lax
from jax.experimental import pallas as pl
from jax.experimental.pallas import tpu as pltpu
from jax.sharding import PartitionSpec as P

F32 = jnp.float32
BF16 = jnp.bfloat16
HIGHEST = lax.Precision.HIGHEST

NR, NC = 8, 16
ND = NR * NC
LAT = 512
WIDTH = 512
KH = 128
ROWS = 4
FRAMES = 4


def far_first():
    offsets = [o for o in itertools.product(range(4), range(2), range(2), range(4), range(2)) if any(o)]
    random.Random(1).shuffle(offsets)
    y_hops = {(0, 0): 0, (1, 0): 1, (0, 1): 2, (1, 1): 1}
    return sorted(offsets, key=lambda o: -(min(o[0], 4 - o[0]) + min(o[3], 4 - o[3]) + y_hops[o[1], o[2]]))


PEERS = far_first()
COT_FIRST = 48
OUT_FIRST = 80
VMEM_LIMIT = 44 * 1024 * 1024
EPS = 1e-05
FACTOR = LAT ** (-0.5)
CUBE = 0.044715
ROOT = math.sqrt(2.0 / math.pi)


def tables():
    n = np.arange(LAT)
    k = np.arange(ND)
    angle = ((k[:, None] * n[None, :]) % LAT).astype(np.float32) * np.float32(2.0 * math.pi / LAT)
    fwd = np.stack([np.cos(angle.astype(np.float64)), -np.sin(angle.astype(np.float64))]).astype(np.float32)
    inv = fwd * np.where(k == 0, 1.0, 2.0).astype(np.float32)[None, :, None]
    order = lambda t: t.reshape(2, 32, 4, LAT).transpose(2, 0, 1, 3).reshape(256, LAT).astype(ml_dtypes.bfloat16)
    m = np.arange(KH) - KH // 2
    u = (np.mod(m[:, None] * n[None, :], LAT)).astype(np.float32) * np.float32(2.0 * math.pi / LAT)
    cos, sin = np.cos(u.astype(np.float64)), np.sin(u.astype(np.float64))
    rot = np.concatenate([np.stack([cos, sin], -1), np.stack([-sin, cos], -1)], 0)
    rot = rot.astype(np.float32).reshape(2 * KH, 2 * LAT).astype(ml_dtypes.bfloat16)
    wf, wi = order(fwd), order(inv)
    place = np.zeros((16, 48, 144), np.float32)
    for y in range(4):
        for x in range(4):
            for part in range(3):
                for tap in range(9):
                    place[4 * y + x, 16 * part + tap, 48 * part + 8 * (y + tap // 3) + x + tap % 3] = 1.0
                place[4 * y + x, 16 * part + 9, 48 * part + 6] = 1.0
    return wf, wi, np.ascontiguousarray(wf.T), np.ascontiguousarray(wi.T), rot, np.ascontiguousarray(rot.T), place.astype(ml_dtypes.bfloat16)


def dot(a, b, precision=None):
    return jnp.dot(a, b, preferred_element_type=F32, precision=precision)


def dot_t(a, b, dims, precision=None):
    return lax.dot_general(a, b, (dims, ((), ())), preferred_element_type=F32, precision=precision)


def gelu_pair(v):
    squared = v * v
    t = jnp.tanh(ROOT * (v + CUBE * (squared * v)))
    half = 0.5 * (1.0 + t)
    slope = half + 0.5 * v * (1.0 - t * t) * (ROOT * (1.0 + (3.0 * CUBE) * squared))
    return v * half, slope


def kernel(
    frames_h, taps_h, bias_h, proj_h, w_in_h, b_in_h, gain_h, lbias_h, w1_h, b1_h, w2_h, b2_h, cot_h,
    wf_h, wi_h, wft_h, wit_h, rot_h, rott_h, place_h,
    den_hbm, agw_out, agf_out,
    frames, taps, bias, proj, w_in, b_in, gain, lbias, w1, b1, w2, b2, cot, wf, wi, wft, wit, rot, rott, place,
    ft, fsend, htop, hbot, frecv, rtop, rbot, est, wbig, projt, tp, lat, emb, nrm, istd, den,
    stage, snd, rcv, wc1, wc2, bc, wsend, wrecv, agw, fsnd, fpair, fsum, frcv, agf,
    isem, lsem, fss, frs, hss, hrs, ass, ars, als, wss, wrs, gss, grs, rss, rrs, qss, qrs, pss, prs,
):
    r = lax.axis_index("rows")
    c = lax.axis_index("cols")
    me = r * NC + c
    kg = me // 4
    cg = lax.rem(me, 4)
    core = lax.rem(c, 2)
    chip = me // 2
    partner = me + 1 - 2 * core

    barrier = pltpu.get_barrier_semaphore()

    @pl.loop(1, NR)
    def _(a):
        row = lax.rem(r + a, NR) * NC
        for k in range(NC):
            pl.semaphore_signal(barrier, inc=1, device_id=row + k, device_id_type=pl.DeviceIdType.LOGICAL)

    for k in range(1, NC):
        pl.semaphore_signal(
            barrier, inc=1, device_id=r * NC + lax.rem(c + k, NC), device_id_type=pl.DeviceIdType.LOGICAL)

    inputs = {}
    for i, (src, dst) in enumerate((
            (frames_h, frames), (cot_h, cot), (wi_h, wi), (taps_h, taps), (bias_h, bias), (place_h, place), (proj_h, proj),
            (w1_h, w1), (w2_h, w2), (b1_h, b1), (b2_h, b2), (w_in_h, w_in), (b_in_h, b_in), (gain_h, gain),
            (lbias_h, lbias), (wf_h, wf), (rot_h, rot), (rott_h, rott), (wit_h, wit), (wft_h, wft))):
        inputs[i] = pltpu.make_async_copy(src, dst, isem.at[i])
        inputs[i].start()

    def arrive(*which):
        for i in which:
            inputs[i].wait()

    at_z = [lax.rem(lax.rem(r, 4) + i, 4) * NC for i in range(4)]
    at_yl = [lax.rem(r // 4 + i, 2) * 4 * NC for i in range(2)]
    at_yh = [lax.rem(c // 8 + i, 2) * 8 for i in range(2)]
    at_x = [lax.rem(lax.rem(c // 2, 4) + i, 4) * 2 for i in range(4)]
    at_core = [core, 1 - core]
    at_row = {(z, yl): at_z[z] + at_yl[yl] for z in range(4) for yl in range(2)}
    at_col = {(yh, x, k): at_yh[yh] + at_x[x] + at_core[k] for yh in range(2) for x in range(4) for k in range(2)}

    def every_peer(act, part=slice(None)):
        for z, yl, yh, x, k in PEERS[part]:
            act(at_row[z, yl] + at_col[yh, x, k])

    def every_chip(act):
        for z, yl, yh, x, k in PEERS:
            if k == 0:
                act(at_row[z, yl] + at_col[yh, x, k])

    def remote(src, dst, ss, rs, d):
        return pltpu.make_async_remote_copy(src, dst, ss, rs, device_id=d, device_id_type=pl.DeviceIdType.LOGICAL)

    def batch(ref, ss, rs):
        return remote(ref, ref, ss, rs, partner)

    zero8 = jnp.zeros((8, 128), F32)
    arrive(0)
    for f in range(FRAMES):
        ft[f, 0:8, :] = zero8
        ft[f, 264:272, :] = zero8
        ft[f, 8:264, :] = frames[f].astype(F32)
    for f in range(FRAMES):
        for j in range(NC):
            fsend[j, f] = ft[f, 16 * j + 7 : 16 * j + 31, :].reshape(3, 8, 128).astype(BF16)
        htop[f] = ft[f, 263:271, :].astype(BF16)
        hbot[f] = ft[f, 7:15, :].astype(BF16)

    def put_rows(h, value):
        for k4 in range(4):
            for p in range(2):
                rows = value[k4 * 64 + p * 32 : k4 * 64 + p * 32 + 32, :]
                for g in range(4):
                    stage[k4, pl.ds(8 * g + 2 * h + p, 32, stride=32), :] = rows[:, 128 * g : 128 * g + 128]

    def pack(e):
        for k4 in range(4):
            snd[e, :, :, 128 * k4 : 128 * k4 + 128] = stage[k4].reshape(ND, 8, 128).astype(BF16)

    def send_own(e):
        pltpu.make_async_copy(snd.at[e, me], rcv.at[e, me], als.at[e]).start()

    def send_all(e, part=slice(None)):
        every_peer(lambda d: remote(snd.at[e, d], rcv.at[e, me], ass.at[e], ars.at[e], d).start(), part)

    def recv_all(e):
        pltpu.make_async_copy(snd.at[e, me], rcv.at[e, me], als.at[e]).wait()
        batch(rcv.at[e, pl.ds(0, ND - 1)], ass.at[e], ars.at[e]).wait_recv()

    arrive(1, 2)
    for h in range(ROWS):
        put_rows(h, dot(wi[...], cot[h]) * FACTOR)
    pack(0)

    arrive(3, 4, 5, 6, 7, 8, 9, 10)
    tp[...] = jnp.zeros(tp.shape, F32)
    tp[0:9, :] = taps[...]
    tp[9:10, :] = bias[...]
    whole = tp[...]
    high = whole.astype(BF16)
    rest = whole - high.astype(F32)
    mid = rest.astype(BF16)
    low = (rest - mid.astype(F32)).astype(BF16)
    parts = jnp.concatenate([high, mid, low], axis=0)
    for yx in range(16):
        wbig[32 * yx : 32 * yx + 32, :] = dot_t(parts, place[yx], ((0,), (0,))).astype(BF16)
    row = lax.broadcasted_iota(jnp.int32, (512, 512), 0)
    col = lax.broadcasted_iota(jnp.int32, (512, 512), 1)
    to_yxc = (row == (col & 31) * 16 + (col >> 5)).astype(F32).astype(BF16)
    projt[...] = dot(proj[...], to_yxc).astype(BF16)
    to_phase = (row == (col & 127) * 4 + (col >> 7)).astype(F32).astype(BF16)
    for wc, w in ((wc1, w1), (wc2, w2)):
        wc[...] = jnp.zeros(wc.shape, F32)
        for b in range(2):
            real = w[0, 2 * cg + b]
            imag = w[1, 2 * cg + b]
            lo, hi = 64 * b, 64 * b + 64
            wc[lo:hi, lo:hi] = real
            wc[128 + lo : 128 + hi, 128 + lo : 128 + hi] = real
            wc[lo:hi, 128 + lo : 128 + hi] = imag
            wc[128 + lo : 128 + hi, lo:hi] = -imag
    lanes = pl.ds(pl.multiple_of(cg * 128, 128), 128)
    bias1 = jnp.concatenate([b1[0:1, lanes], b1[1:2, lanes]], axis=1)
    bias2 = jnp.concatenate([b2[0:1, lanes], b2[1:2, lanes]], axis=1)
    for f in range(FRAMES):
        for t in range(4):
            est[f, t, pl.ds(6, 24, stride=8), :] = jnp.ones((24, 128), F32)
            est[f, t, pl.ds(7, 24, stride=8), :] = jnp.zeros((24, 128), F32)

    pl.semaphore_wait(barrier, ND - 1)

    @pl.loop(1, NC)
    def _(i):
        j = lax.rem(c + i, NC)
        remote(fsend.at[j], frecv.at[c], fss, frs, r * NC + j).start()

    own_frames = pltpu.make_async_copy(fsend.at[c], frecv.at[c], lsem.at[1])
    own_frames.start()

    @pl.when(r < NR - 1)
    def _():
        remote(htop, rtop.at[c], hss.at[0], hrs.at[0], (r + 1) * NC).start()

    @pl.when(r > 0)
    def _():
        remote(hbot, rbot.at[c], hss.at[1], hrs.at[1], r * NC - 1).start()

    has_top = jnp.logical_and(c == 0, r > 0)
    has_bot = jnp.logical_and(c == NC - 1, r < NR - 1)

    @pl.when(jnp.logical_not(has_top))
    def _():
        rtop[...] = jnp.zeros(rtop.shape, BF16)

    @pl.when(jnp.logical_not(has_bot))
    def _():
        rbot[...] = jnp.zeros(rbot.shape, BF16)

    send_own(0)
    send_all(0, slice(0, COT_FIRST))

    own_frames.wait()
    batch(frecv.at[pl.ds(0, NC - 1)], fss, frs).wait_recv()

    @pl.when(has_top)
    def _():
        batch(rtop, hss.at[0], hrs.at[0]).wait_recv()

    @pl.when(has_bot)
    def _():
        batch(rbot, hss.at[1], hrs.at[1]).wait_recv()

    send_all(0, slice(COT_FIRST, None))
    split = []
    for g in range(4):
        pieces = []
        for j in range(4):
            v = frecv[4 * g + j].astype(F32)
            up = v[:, 0] + rtop[4 * g + j].astype(F32)
            down = v[:, 2] + rbot[4 * g + j].astype(F32)
            pieces.append(jnp.stack([up, v[:, 1], down], axis=1).reshape(96, 128).astype(BF16))
        split.append(dot(jnp.concatenate(pieces, axis=1), to_phase))
    lane = lax.broadcasted_iota(jnp.int32, (96, 512), 1)
    first = jnp.concatenate([s[:, 0:128] for s in split], axis=1)
    last = jnp.concatenate([s[:, 384:512] for s in split], axis=1)
    before = jnp.where(lane == 0, 0.0, pltpu.roll(last, 1, axis=1))
    after = jnp.where(lane == LAT - 1, 0.0, pltpu.roll(first, LAT - 1, axis=1))
    for t in range(4):
        own = slice(128 * t, 128 * t + 128)
        planes = [before[:, own]] + [split[t][:, 128 * q : 128 * q + 128] for q in range(4)] + [after[:, own]]
        for x, plane in enumerate(planes):
            for f in range(FRAMES):
                est[f, t, pl.ds(x, 24, stride=8), :] = plane[24 * f : 24 * f + 24, :]

    @pl.loop(0, ROWS)
    def _(h):
        for f in range(FRAMES):
            top = pl.multiple_of(32 * h, 32)
            patch = jnp.concatenate([est[f, t, pl.ds(top, 48), :] for t in range(4)], axis=1).astype(BF16)
            hidden = dot(wbig[...], jnp.concatenate([patch, patch, patch], axis=0))
            hidden = jnp.maximum(hidden, 0.0).astype(BF16)
            lat[h, 32 * f : 32 * f + 32, :] = dot(projt[...], hidden).astype(BF16)

    arrive(11, 12, 13, 14, 15)
    for h in range(ROWS):
        embedded = dot_t(lat[h], w_in[...], ((0,), (0,))) + b_in[...]
        emb[h] = embedded
        centered = embedded - jnp.mean(embedded, axis=1, keepdims=True)
        inverse = lax.rsqrt(jnp.mean(centered * centered, axis=1, keepdims=True) + EPS)
        normalized = centered * inverse
        istd[h] = inverse
        nrm[h] = normalized
        normed = (normalized * gain[...] + lbias[...]).astype(BF16)
        put_rows(h, dot(wf[...], normed) * FACTOR)
    pack(1)
    send_own(1)
    send_all(1)

    def to_modes(e):
        x = rcv[e].astype(F32).reshape(2 * LAT, 512).astype(BF16)
        return stacked(dot(rot[...], x) * FACTOR)

    def stacked(v):
        return jnp.concatenate(
            [jnp.concatenate([v[0:KH, 128 * q : 128 * q + 128], v[KH:, 128 * q : 128 * q + 128]], axis=1) for q in range(4)], axis=0)

    def unstacked(v):
        return jnp.concatenate(
            [jnp.concatenate([v[KH * q : KH * q + KH, 128 * p : 128 * p + 128] for q in range(4)], axis=1) for p in range(2)], axis=0)

    def from_modes(e, v, part=slice(None)):
        back = dot(rott[...], unstacked(v).astype(BF16)) * FACTOR
        snd[e] = back.reshape(ND, 8, 512).astype(BF16)
        send_own(e)
        send_all(e, part)

    arrive(16, 17, 18, 19)
    recv_all(0)
    grad = to_modes(0)
    grad_act = dot_t(grad, wc2[...], ((1,), (1,)), HIGHEST)
    recv_all(1)
    coeffs = to_modes(1)
    pre = dot(coeffs, wc1[...], HIGHEST) + bias1
    act, slope = gelu_pair(pre)
    back = grad_act * slope
    from_modes(3, dot_t(back, wc1[...], ((1,), (1,)), HIGHEST))

    half = lax.broadcasted_iota(jnp.int32, (64, 128), 1) < 64

    def weight_grad(left, right):
        g = dot_t(left, right, ((0,), (0,)), HIGHEST)
        real = g[0:128, 0:128] + g[128:256, 128:256]
        imag = g[0:128, 128:256] - g[128:256, 0:128]
        return [jnp.where(half, v[0:64, :], v[64:128, :]) for v in (real, imag)]

    tiles = weight_grad(coeffs, back) + weight_grad(act, grad)
    wsend[...] = jnp.concatenate(tiles, axis=0).reshape(32, 8, 128)
    wrecv[kg] = wsend[kg]

    @pl.loop(1, 32)
    def _(i):
        j = lax.rem(kg + i, 32)
        remote(wsend.at[j], wrecv.at[kg], wss, wrs, 4 * j + cg).start()

    from_modes(2, dot(act, wc2[...], HIGHEST) + bias2, slice(0, OUT_FIRST))

    sum1 = jnp.sum(back, axis=0, keepdims=True)
    sum2 = jnp.sum(grad, axis=0, keepdims=True)
    bc[...] = jnp.zeros(bc.shape, F32)
    for p in range(2):
        bc[p : p + 1, lanes] = sum1[:, 128 * p : 128 * p + 128]
        bc[2 + p : 3 + p, lanes] = sum2[:, 128 * p : 128 * p + 128]

    def get_rows(e, h):
        blocks = []
        for k4 in range(4):
            for q in range(2):
                blocks.append(jnp.concatenate(
                    [stage[k4, pl.ds(8 * g + 2 * h + q, 32, stride=32), :] for g in range(4)], axis=1))
        return jnp.concatenate(blocks, axis=0).astype(BF16)

    def unpack(e):
        for k4 in range(4):
            stage[k4] = rcv[e, :, :, 128 * k4 : 128 * k4 + 128].astype(F32).reshape(8 * ND, 128)

    recv_all(3)
    batch(wrecv.at[pl.ds(0, 31)], wss, wrs).wait_recv()
    agw[core, kg, lax.rem(chip, 2)] = jnp.sum(wrecv[...], axis=0)
    mine = agw.at[core, kg, lax.rem(chip, 2)]
    every_chip(lambda d: remote(mine, mine, gss, grs, d).start())

    unpack(3)
    sums = [jnp.zeros((1, WIDTH), F32) for _ in range(3)]
    weight = jnp.zeros((128, WIDTH), F32)
    for h in range(ROWS):
        gn = dot(wft[...], get_rows(3, h)) * FACTOR
        normalized = nrm[h]
        sums[1] = sums[1] + jnp.sum(gn * normalized, axis=0, keepdims=True)
        sums[2] = sums[2] + jnp.sum(gn, axis=0, keepdims=True)
        scaled = gn * gain[...]
        ge = cot[h].astype(F32) + istd[h] * (
            scaled
            - jnp.mean(scaled, axis=1, keepdims=True)
            - normalized * jnp.mean(scaled * normalized, axis=1, keepdims=True))
        sums[0] = sums[0] + jnp.sum(ge, axis=0, keepdims=True)
        weight = weight + dot(lat[h], ge.astype(BF16))

    for a in range(32):
        for b in range(4):
            own = slice(128 * b, 128 * b + 128)
            at = (b % 2, 2 * a + b // 2)
            fsnd[at[0], at[1], 0:4, :] = weight[4 * a : 4 * a + 4, own]
            if a < 3:
                fsnd[at[0], at[1], 4:5, :] = sums[a][:, own]
            elif a < 7:
                fsnd[at[0], at[1], 4:5, :] = bc[a - 3 : a - 2, own]
            else:
                fsnd[at[0], at[1], 4:5, :] = jnp.zeros((1, 128), F32)
            fsnd[at[0], at[1], 5:8, :] = jnp.zeros((3, 128), F32)
    remote(fsnd.at[1 - core], fpair, pss.at[0], prs.at[0], partner).start()
    batch(fpair, pss.at[0], prs.at[0]).wait_recv()
    fsum[...] = fsnd[core] + fpair[...]
    frcv[chip] = fsum[chip]
    every_chip(lambda d: remote(fsum.at[d // 2], frcv.at[chip], rss, rrs, d).start())

    send_all(2, slice(OUT_FIRST, None))

    batch(frcv.at[pl.ds(0, 63)], rss, rrs).wait_recv()
    agf[core, chip] = jnp.sum(frcv[...], axis=0)
    every_chip(lambda d: remote(agf.at[core, chip], agf.at[core, chip], qss, qrs, d).start())

    recv_all(2)
    unpack(2)
    for h in range(ROWS):
        den[h] = (emb[h] + dot(wit[...], get_rows(2, h)) * FACTOR).astype(BF16)
        pltpu.make_async_copy(den.at[h], den_hbm.at[h], lsem.at[2 + h]).start()

    batch(frcv.at[pl.ds(0, 63)], gss, grs).wait_recv()
    remote(agw.at[core], agw.at[core], pss.at[1], prs.at[1], partner).start()
    batch(frcv.at[pl.ds(0, 63)], qss, qrs).wait_recv()
    remote(agf.at[core], agf.at[core], pss.at[2], prs.at[2], partner).start()
    batch(agw.at[0], pss.at[1], prs.at[1]).wait_recv()
    agw_copy = pltpu.make_async_copy(agw, agw_out, lsem.at[6])
    agw_copy.start()
    batch(agf.at[0], pss.at[2], prs.at[2]).wait_recv()
    agf_copy = pltpu.make_async_copy(agf, agf_out, lsem.at[7])
    agf_copy.start()

    agw_copy.wait()
    agf_copy.wait()
    for h in range(ROWS):
        pltpu.make_async_copy(den.at[h], den_hbm.at[h], lsem.at[2 + h]).wait()
    batch(frecv.at[pl.ds(0, NC - 1)], fss, frs).wait_send()

    @pl.when(r < NR - 1)
    def _():
        batch(htop, hss.at[0], hrs.at[0]).wait_send()

    @pl.when(r > 0)
    def _():
        batch(hbot, hss.at[1], hrs.at[1]).wait_send()

    for e in range(4):
        batch(rcv.at[e, pl.ds(0, ND - 1)], ass.at[e], ars.at[e]).wait_send()
    batch(wrecv.at[pl.ds(0, 31)], wss, wrs).wait_send()
    batch(fpair, pss.at[0], prs.at[0]).wait_send()
    batch(agw.at[0], pss.at[1], prs.at[1]).wait_send()
    batch(agf.at[0], pss.at[2], prs.at[2]).wait_send()
    for ss, rs in ((gss, grs), (rss, rrs), (qss, qrs)):
        batch(frcv.at[pl.ds(0, 63)], ss, rs).wait_send()


def finish(den_in, agw, agf, den_out, gwin, gbin, ggain, gbias, gw1, gb1, gw2, gb2, sem):
    outs = [pltpu.make_async_copy(den_in.at[h], den_out.at[h], sem.at[h]) for h in range(ROWS)]
    for copy in outs:
        copy.start()
    for w, gw in enumerate((gw1, gw2)):
        for p in range(2):
            for g in range(4):
                v = agw[g % 2, 16 * w + 8 * p : 16 * w + 8 * p + 8, g // 2].reshape(64, 128)
                gw[p, 2 * g] = v[:, 0:64]
                gw[p, 2 * g + 1] = v[:, 64:128]
    small = (gbin, ggain, gbias)
    for b in range(4):
        own = slice(128 * b, 128 * b + 128)
        for a in range(32):
            gwin[4 * a : 4 * a + 4, own] = agf[b % 2, 2 * a + b // 2, 0:4, :]
        for a in range(3):
            small[a][:, own] = agf[b % 2, 2 * a + b // 2, 4:5, :]
        for a in range(2):
            gb1[a : a + 1, own] = agf[b % 2, 2 * (a + 3) + b // 2, 4:5, :]
            gb2[a : a + 1, own] = agf[b % 2, 2 * (a + 5) + b // 2, 4:5, :]
    for copy in outs:
        copy.wait()


def body(frames, enc_taps, enc_bias, enc_proj, w_in, b_in, ln_gain, ln_bias, spec_w1, spec_b1, spec_w2, spec_b2, cotangent):
    vmem = pl.BlockSpec(memory_space=pltpu.VMEM)
    hbm = pl.BlockSpec(memory_space=pltpu.HBM)
    anywhere = pl.BlockSpec(memory_space=pl.ANY)
    shape = jax.ShapeDtypeStruct
    dma = pltpu.SemaphoreType.DMA
    operands = (
        frames, enc_taps, enc_bias.reshape(1, -1), enc_proj.T, w_in, b_in.reshape(1, -1), ln_gain.reshape(1, -1),
        ln_bias.reshape(1, -1), spec_w1, spec_b1, spec_w2, spec_b2, cotangent) + tuple(jnp.asarray(t) for t in tables())
    den, agw, agf = pl.pallas_call(
        kernel,
        out_shape=(shape((ROWS, LAT, WIDTH), BF16), shape((2, 32, 2, 8, 128), F32), shape((2, 64, 8, 128), F32)),
        in_specs=[hbm] * 20,
        out_specs=(anywhere, anywhere, anywhere),
        scratch_shapes=[pltpu.VMEM(x.shape, x.dtype) for x in operands] + [
            pltpu.VMEM((FRAMES, 272, 128), F32),
            pltpu.VMEM((NC, FRAMES, 3, 8, 128), BF16),
            pltpu.VMEM((FRAMES, 8, 128), BF16),
            pltpu.VMEM((FRAMES, 8, 128), BF16),
            pltpu.VMEM((NC, FRAMES, 3, 8, 128), BF16),
            pltpu.VMEM((NC, FRAMES, 8, 128), BF16),
            pltpu.VMEM((NC, FRAMES, 8, 128), BF16),
            pltpu.VMEM((FRAMES, 4, 192, 128), F32),
            pltpu.VMEM((512, 144), BF16),
            pltpu.VMEM((32, 512), BF16),
            pltpu.VMEM((16, 32), F32),
            pltpu.VMEM((ROWS, 128, LAT), BF16),
            pltpu.VMEM((ROWS, LAT, WIDTH), F32),
            pltpu.VMEM((ROWS, LAT, WIDTH), F32),
            pltpu.VMEM((ROWS, LAT, 1), F32),
            pltpu.VMEM((ROWS, LAT, WIDTH), BF16),
            pltpu.VMEM((4, 8 * ND, 128), F32),
            pltpu.VMEM((4, ND, 8, 512), BF16),
            pltpu.VMEM((4, ND, 8, 512), BF16),
            pltpu.VMEM((256, 256), F32),
            pltpu.VMEM((256, 256), F32),
            pltpu.VMEM((8, WIDTH), F32),
            pltpu.VMEM((32, 8, 128), F32),
            pltpu.VMEM((32, 8, 128), F32),
            pltpu.VMEM((2, 32, 2, 8, 128), F32),
            pltpu.VMEM((2, 64, 8, 128), F32),
            pltpu.VMEM((64, 8, 128), F32),
            pltpu.VMEM((64, 8, 128), F32),
            pltpu.VMEM((64, 8, 128), F32),
            pltpu.VMEM((2, 64, 8, 128), F32),
            dma((20,)), dma((8,)), dma(()), dma(()), dma((2,)), dma((2,)), dma((4,)), dma((4,)), dma((4,)),
            dma(()), dma(()), dma(()), dma(()), dma(()), dma(()), dma(()), dma(()), dma((3,)), dma((3,)),
        ],
        compiler_params=pltpu.CompilerParams(
            collective_id=0, has_side_effects=True, vmem_limit_bytes=VMEM_LIMIT),
        name="step",
    )(*(pltpu.with_memory_space_constraint(x, pltpu.HBM) for x in operands))
    den, gwin, gbin, ggain, gbias, gw1, gb1, gw2, gb2 = pl.pallas_call(
        finish,
        out_shape=(
            shape((ROWS, LAT, WIDTH), BF16), shape((128, WIDTH), F32), shape((1, WIDTH), F32), shape((1, WIDTH), F32),
            shape((1, WIDTH), F32), shape((2, 8, 64, 64), F32), shape((2, WIDTH), F32), shape((2, 8, 64, 64), F32),
            shape((2, WIDTH), F32)),
        in_specs=[vmem] * 3,
        out_specs=(hbm,) + (vmem,) * 8,
        scratch_shapes=[dma((ROWS,))],
        compiler_params=pltpu.CompilerParams(vmem_limit_bytes=16 * 1024 * 1024),
        name="finish",
    )(den, agw, agf)
    return (den, gwin, gbin.reshape(-1), ggain.reshape(-1), gbias.reshape(-1), gw1, gb1, gw2, gb2)


def solution(mesh):
    return jax.shard_map(
        body,
        mesh=mesh,
        in_specs=(P(None, "rows", "cols"),) + (P(),) * 11 + (P(("rows", "cols"), None, None),),
        out_specs=(P(("rows", "cols"), None, None),) + (P(),) * 8,
        check_vma=False,
    )
```

time: 121 us -> 98.6 us (0.81)
  Pallas kernels: 110 us -> 97.6 us
  local copies, waits for them, and re-layouts: 9.9 us -> 0 us
    pallas_call x1, Pallas kernels: 110 us -> 95.2 us  [body(): pl.pallas_call(kernel, out_shape=(shape((ROWS, LAT, WIDTH), BF16), shape(...]
    unnamed x26 -> x0, local copies, waits for them, and re-layouts: 9.9 us -> none
    pallas_call x0 -> x1, Pallas kernels: none -> 2.44 us  [body(): pl.pallas_call(finish, out_shape=(shape((ROWS, LAT, WIDTH), BF16), shape(...]
where the time goes in v2:
time: 98.6 us; the launch traced here: 98.5 us
  Pallas kernels  97.6 us (99%)
    pallas_call x1, Pallas kernels, body(): pl.pallas_call(kernel, out_shape=(shape((ROWS, LAT, WIDTH), BF16), shape(...  95.2 us
    pallas_call x1, Pallas kernels, body(): pl.pallas_call(finish, out_shape=(shape((ROWS, LAT, WIDTH), BF16), shape(...  2.44 us

profile of v2, /device:TPU:1, one launch (start us, length us, event | category | flops | bytes accessed | tf_op | source)
XLA Modules:
  0.0 98.5 jit_solution(16639123978154724370)
XLA Ops:
  0.6 95.2 %step.1 = (bf16[4,512,512]{2,1,0:T(8,128)(2,1)S(1)}, f32[2,32,2,8,128]{4,3,2,1,0:T(8,128)S(1)}, f32[2,64,8,128]{3,2,1,0:T(8,128)S(1)}) custom-call(bf16[4,256,128]{2,1,0:T(8,128)(2,1)} %frames_h.1, f32[9,32]{1,0:T(8,128)} %taps_h.1, f32[1,32]{1,0:T(1,128)} %bitcast.12, bf16[32,512]{1,0:T(8,128)(2,1)} %bitcast.8, bf16[128,512]{1,0:T(8,128)(2,1)} %w_in_h.1, ...), custom_call_target="tpu_custom_call" | custom-call | tf_op jit(solution)/shard_map/step/pallas_call | solution.py:497
  95.8 2.4 %finish.1 = (bf16[4,512,512]{2,1,0:T(8,128)(2,1)}, f32[128,512]{1,0:T(8,128)}, f32[1,512]{1,0:T(1,128)}, f32[1,512]{1,0:T(1,128)}, f32[1,512]{1,0:T(1,128)}, /*i...) custom-call(bf16[4,512,512]{2,1,0:T(8,128)(2,1)S(1)} %get-tuple-element.21.den_in, ...), custom_call_target="tpu_custom_call" | custom-call | tf_op jit(solution)/shard_map/finish/pallas_call | solution.py:540

commit v3 on v2

--- a/solution.py
+++ b/solution.py
@@ -32,8 +32,9 @@
 
 
 PEERS = far_first()
-COT_FIRST = 48
-OUT_FIRST = 80
+OUT_FIRST = 24
+OUT_SECOND = 24
+SUMS_AT = 4
 VMEM_LIMIT = 44 * 1024 * 1024
 EPS = 1e-05
 FACTOR = LAT ** (-0.5)
@@ -83,11 +84,11 @@
 def kernel(
     frames_h, taps_h, bias_h, proj_h, w_in_h, b_in_h, gain_h, lbias_h, w1_h, b1_h, w2_h, b2_h, cot_h,
     wf_h, wi_h, wft_h, wit_h, rot_h, rott_h, place_h,
-    den_hbm, agw_out, agf_out,
+    den_hbm, agw_out, agf_out, agt_out,
     frames, taps, bias, proj, w_in, b_in, gain, lbias, w1, b1, w2, b2, cot, wf, wi, wft, wit, rot, rott, place,
     ft, fsend, htop, hbot, frecv, rtop, rbot, est, wbig, projt, tp, lat, emb, nrm, istd, den,
-    stage, snd, rcv, wc1, wc2, bc, wsend, wrecv, agw, fsnd, fpair, fsum, frcv, agf,
-    isem, lsem, fss, frs, hss, hrs, ass, ars, als, wss, wrs, gss, grs, rss, rrs, qss, qrs, pss, prs,
+    stage, snd, rcv, wc1, wc2, bc, wsend, wrecv, agw, fsnd, fpair, fsum, frcv, agf, tiny, tpair, tsum, trcv, agt,
+    isem, lsem, fss, frs, hss, hrs, ass, ars, als, wss, wrs, gss, grs, rss, rrs, qss, qrs, pss, prs, tss, trs, uss, urs,
 ):
     r = lax.axis_index("rows")
     c = lax.axis_index("cols")
@@ -97,6 +98,7 @@
     core = lax.rem(c, 2)
     chip = me // 2
     partner = me + 1 - 2 * core
+    owner = (13 + 24 * core, 50 - 24 * core)
 
     barrier = pltpu.get_barrier_semaphore()
 
@@ -201,15 +203,19 @@
     projt[...] = dot(proj[...], to_yxc).astype(BF16)
     to_phase = (row == (col & 127) * 4 + (col >> 7)).astype(F32).astype(BF16)
     for wc, w in ((wc1, w1), (wc2, w2)):
-        wc[...] = jnp.zeros(wc.shape, F32)
+        wc[...] = jnp.zeros(wc.shape, BF16)
         for b in range(2):
-            real = w[0, 2 * cg + b]
-            imag = w[1, 2 * cg + b]
             lo, hi = 64 * b, 64 * b + 64
-            wc[lo:hi, lo:hi] = real
-            wc[128 + lo : 128 + hi, 128 + lo : 128 + hi] = real
-            wc[lo:hi, 128 + lo : 128 + hi] = imag
-            wc[128 + lo : 128 + hi, lo:hi] = -imag
+            for p in range(2):
+                whole = w[p, 2 * cg + b]
+                high = whole.astype(BF16)
+                for i, v in enumerate((high, (whole - high.astype(F32)).astype(BF16))):
+                    if p == 0:
+                        wc[i, lo:hi, lo:hi] = v
+                        wc[i, 128 + lo : 128 + hi, 128 + lo : 128 + hi] = v
+                    else:
+                        wc[i, lo:hi, 128 + lo : 128 + hi] = v
+                        wc[i, 128 + lo : 128 + hi, lo:hi] = -v
     lanes = pl.ds(pl.multiple_of(cg * 128, 128), 128)
     bias1 = jnp.concatenate([b1[0:1, lanes], b1[1:2, lanes]], axis=1)
     bias2 = jnp.concatenate([b2[0:1, lanes], b2[1:2, lanes]], axis=1)
@@ -220,9 +226,7 @@
 
     pl.semaphore_wait(barrier, ND - 1)
 
-    @pl.loop(1, NC)
-    def _(i):
-        j = lax.rem(c + i, NC)
+    for j in [at_col[yh, x, k] for z, yl, yh, x, k in PEERS if z == yl == 0]:
         remote(fsend.at[j], frecv.at[c], fss, frs, r * NC + j).start()
 
     own_frames = pltpu.make_async_copy(fsend.at[c], frecv.at[c], lsem.at[1])
@@ -248,7 +252,6 @@
         rbot[...] = jnp.zeros(rbot.shape, BF16)
 
     send_own(0)
-    send_all(0, slice(0, COT_FIRST))
 
     own_frames.wait()
     batch(frecv.at[pl.ds(0, NC - 1)], fss, frs).wait_recv()
@@ -261,7 +264,7 @@
     def _():
         batch(rbot, hss.at[1], hrs.at[1]).wait_recv()
 
-    send_all(0, slice(COT_FIRST, None))
+    send_all(0)
     split = []
     for g in range(4):
         pieces = []
@@ -308,7 +311,7 @@
     send_all(1)
 
     def to_modes(e):
-        x = rcv[e].astype(F32).reshape(2 * LAT, 512).astype(BF16)
+        x = rcv[e].reshape(2 * LAT, 512)
         return stacked(dot(rot[...], x) * FACTOR)
 
     def stacked(v):
@@ -319,22 +322,28 @@
         return jnp.concatenate(
             [jnp.concatenate([v[KH * q : KH * q + KH, 128 * p : 128 * p + 128] for q in range(4)], axis=1) for p in range(2)], axis=0)
 
-    def from_modes(e, v, part=slice(None)):
+    def to_back(e, v):
         back = dot(rott[...], unstacked(v).astype(BF16)) * FACTOR
         snd[e] = back.reshape(ND, 8, 512).astype(BF16)
-        send_own(e)
-        send_all(e, part)
+
+    def dot3(v, wc, side=0):
+        high = v.astype(BF16)
+        low = (v - high.astype(F32)).astype(BF16)
+        dims = ((1,), (side,))
+        return dot_t(high, wc[0], dims) + (dot_t(high, wc[1], dims) + dot_t(low, wc[0], dims))
 
     arrive(16, 17, 18, 19)
     recv_all(0)
     grad = to_modes(0)
-    grad_act = dot_t(grad, wc2[...], ((1,), (1,)), HIGHEST)
+    grad_act = dot3(grad, wc2, 1)
     recv_all(1)
     coeffs = to_modes(1)
-    pre = dot(coeffs, wc1[...], HIGHEST) + bias1
+    pre = dot3(coeffs, wc1) + bias1
     act, slope = gelu_pair(pre)
     back = grad_act * slope
-    from_modes(3, dot_t(back, wc1[...], ((1,), (1,)), HIGHEST))
+    to_back(3, dot3(back, wc1, 1))
+    send_own(3)
+    send_all(3)
 
     half = lax.broadcasted_iota(jnp.int32, (64, 128), 1) < 64
 
@@ -353,7 +362,7 @@
         j = lax.rem(kg + i, 32)
         remote(wsend.at[j], wrecv.at[kg], wss, wrs, 4 * j + cg).start()
 
-    from_modes(2, dot(act, wc2[...], HIGHEST) + bias2, slice(0, OUT_FIRST))
+    to_back(2, dot3(act, wc2) + bias2)
 
     sum1 = jnp.sum(back, axis=0, keepdims=True)
     sum2 = jnp.sum(grad, axis=0, keepdims=True)
@@ -375,70 +384,105 @@
             stage[k4] = rcv[e, :, :, 128 * k4 : 128 * k4 + 128].astype(F32).reshape(8 * ND, 128)
 
     recv_all(3)
-    batch(wrecv.at[pl.ds(0, 31)], wss, wrs).wait_recv()
-    agw[core, kg, lax.rem(chip, 2)] = jnp.sum(wrecv[...], axis=0)
+    send_own(2)
+    send_all(2, slice(0, OUT_FIRST))
+    unpack(3)
     mine = agw.at[core, kg, lax.rem(chip, 2)]
-    every_chip(lambda d: remote(mine, mine, gss, grs, d).start())
-
-    unpack(3)
+    wide = trcv.at[0, pl.ds(0, 63)]
+
+    def send_spectral_sums():
+        batch(wrecv.at[pl.ds(0, 31)], wss, wrs).wait_recv()
+        agw[core, kg, lax.rem(chip, 2)] = jnp.sum(wrecv[...], axis=0)
+        every_chip(lambda d: remote(mine, mine, gss, grs, d).start())
+
+    scaled_gain = gain[...] * FACTOR
     sums = [jnp.zeros((1, WIDTH), F32) for _ in range(3)]
     weight = jnp.zeros((128, WIDTH), F32)
     for h in range(ROWS):
-        gn = dot(wft[...], get_rows(3, h)) * FACTOR
+        if SUMS_AT == h:
+            send_spectral_sums()
+        gn = dot(wft[...], get_rows(3, h))
         normalized = nrm[h]
         sums[1] = sums[1] + jnp.sum(gn * normalized, axis=0, keepdims=True)
         sums[2] = sums[2] + jnp.sum(gn, axis=0, keepdims=True)
-        scaled = gn * gain[...]
+        scaled = gn * scaled_gain
         ge = cot[h].astype(F32) + istd[h] * (
             scaled
             - jnp.mean(scaled, axis=1, keepdims=True)
             - normalized * jnp.mean(scaled * normalized, axis=1, keepdims=True))
         sums[0] = sums[0] + jnp.sum(ge, axis=0, keepdims=True)
         weight = weight + dot(lat[h], ge.astype(BF16))
-
-    for a in range(32):
-        for b in range(4):
-            own = slice(128 * b, 128 * b + 128)
-            at = (b % 2, 2 * a + b // 2)
-            fsnd[at[0], at[1], 0:4, :] = weight[4 * a : 4 * a + 4, own]
-            if a < 3:
-                fsnd[at[0], at[1], 4:5, :] = sums[a][:, own]
-            elif a < 7:
-                fsnd[at[0], at[1], 4:5, :] = bc[a - 3 : a - 2, own]
-            else:
-                fsnd[at[0], at[1], 4:5, :] = jnp.zeros((1, 128), F32)
-            fsnd[at[0], at[1], 5:8, :] = jnp.zeros((3, 128), F32)
+    sums = [sums[0], sums[1] * FACTOR, sums[2] * FACTOR]
+
+    for b in range(4):
+        own = slice(128 * b, 128 * b + 128)
+        for a in range(32):
+            fsnd[b % 2, 2 * a + b // 2] = weight[4 * a : 4 * a + 4, own]
+        tiny[b % 2, b // 2] = jnp.concatenate([v[:, own] for v in sums] + [bc[0:4, own], jnp.zeros((1, 128), F32)], axis=0)
     remote(fsnd.at[1 - core], fpair, pss.at[0], prs.at[0], partner).start()
+    remote(tiny.at[1 - core], tpair, pss.at[3], prs.at[3], partner).start()
     batch(fpair, pss.at[0], prs.at[0]).wait_recv()
     fsum[...] = fsnd[core] + fpair[...]
     frcv[chip] = fsum[chip]
     every_chip(lambda d: remote(fsum.at[d // 2], frcv.at[chip], rss, rrs, d).start())
-
-    send_all(2, slice(OUT_FIRST, None))
+    batch(tpair, pss.at[3], prs.at[3]).wait_recv()
+    tsum[...] = tiny[core] + tpair[...]
+    for t in range(2):
+        trcv[t, chip] = tsum[t]
+
+        @pl.when(chip != owner[t])
+        def _():
+            remote(tsum.at[t], trcv.at[t, chip], tss.at[t], trs.at[t], 2 * owner[t] + core).start()
+
+    send_all(2, slice(OUT_FIRST, OUT_SECOND))
+    if SUMS_AT == 4:
+        send_spectral_sums()
 
     batch(frcv.at[pl.ds(0, 63)], rss, rrs).wait_recv()
     agf[core, chip] = jnp.sum(frcv[...], axis=0)
     every_chip(lambda d: remote(agf.at[core, chip], agf.at[core, chip], qss, qrs, d).start())
-
+    for t in range(2):
+
+        @pl.when(chip == owner[t])
+        def _():
+            batch(trcv.at[t, pl.ds(0, 63)], tss.at[t], trs.at[t]).wait_recv()
+            agt[core, t] = jnp.sum(trcv[t], axis=0)
+            every_chip(lambda d: remote(agt.at[core, t], agt.at[core, t], uss.at[t], urs.at[t], d).start())
+
+    if SUMS_AT == 5:
+        send_spectral_sums()
+    send_all(2, slice(OUT_SECOND, None))
+
+    batch(wide, gss, grs).wait_recv()
+    remote(agw.at[core], agw.at[core], pss.at[1], prs.at[1], partner).start()
+    batch(frcv.at[pl.ds(0, 63)], qss, qrs).wait_recv()
+    remote(agf.at[core], agf.at[core], pss.at[2], prs.at[2], partner).start()
+    for t in range(2):
+
+        @pl.when(chip != owner[t])
+        def _():
+            batch(agt.at[core, t], uss.at[t], urs.at[t]).wait_recv()
+
+    remote(agt.at[core], agt.at[core], pss.at[4], prs.at[4], partner).start()
     recv_all(2)
     unpack(2)
     for h in range(ROWS):
         den[h] = (emb[h] + dot(wit[...], get_rows(2, h)) * FACTOR).astype(BF16)
         pltpu.make_async_copy(den.at[h], den_hbm.at[h], lsem.at[2 + h]).start()
 
-    batch(frcv.at[pl.ds(0, 63)], gss, grs).wait_recv()
-    remote(agw.at[core], agw.at[core], pss.at[1], prs.at[1], partner).start()
-    batch(frcv.at[pl.ds(0, 63)], qss, qrs).wait_recv()
-    remote(agf.at[core], agf.at[core], pss.at[2], prs.at[2], partner).start()
     batch(agw.at[0], pss.at[1], prs.at[1]).wait_recv()
     agw_copy = pltpu.make_async_copy(agw, agw_out, lsem.at[6])
     agw_copy.start()
     batch(agf.at[0], pss.at[2], prs.at[2]).wait_recv()
     agf_copy = pltpu.make_async_copy(agf, agf_out, lsem.at[7])
     agf_copy.start()
+    batch(agt.at[0], pss.at[4], prs.at[4]).wait_recv()
+    agt_copy = pltpu.make_async_copy(agt, agt_out, lsem.at[0])
+    agt_copy.start()
 
     agw_copy.wait()
     agf_copy.wait()
+    agt_copy.wait()
     for h in range(ROWS):
         pltpu.make_async_copy(den.at[h], den_hbm.at[h], lsem.at[2 + h]).wait()
     batch(frecv.at[pl.ds(0, NC - 1)], fss, frs).wait_send()
@@ -457,11 +501,23 @@
     batch(fpair, pss.at[0], prs.at[0]).wait_send()
     batch(agw.at[0], pss.at[1], prs.at[1]).wait_send()
     batch(agf.at[0], pss.at[2], prs.at[2]).wait_send()
-    for ss, rs in ((gss, grs), (rss, rrs), (qss, qrs)):
-        batch(frcv.at[pl.ds(0, 63)], ss, rs).wait_send()
-
-
-def finish(den_in, agw, agf, den_out, gwin, gbin, ggain, gbias, gw1, gb1, gw2, gb2, sem):
+    batch(tpair, pss.at[3], prs.at[3]).wait_send()
+    batch(agt.at[0], pss.at[4], prs.at[4]).wait_send()
+    batch(wide, gss, grs).wait_send()
+    batch(frcv.at[pl.ds(0, 63)], rss, rrs).wait_send()
+    batch(frcv.at[pl.ds(0, 63)], qss, qrs).wait_send()
+    for t in range(2):
+
+        @pl.when(chip != owner[t])
+        def _():
+            batch(tsum.at[t], tss.at[t], trs.at[t]).wait_send()
+
+        @pl.when(chip == owner[t])
+        def _():
+            batch(trcv.at[t, pl.ds(0, 63)], uss.at[t], urs.at[t]).wait_send()
+
+
+def finish(den_in, agw, agf, agt, den_out, gwin, gbin, ggain, gbias, gw1, gb1, gw2, gb2, sem):
     outs = [pltpu.make_async_copy(den_in.at[h], den_out.at[h], sem.at[h]) for h in range(ROWS)]
     for copy in outs:
         copy.start()
@@ -471,16 +527,15 @@
                 v = agw[g % 2, 16 * w + 8 * p : 16 * w + 8 * p + 8, g // 2].reshape(64, 128)
                 gw[p, 2 * g] = v[:, 0:64]
                 gw[p, 2 * g + 1] = v[:, 64:128]
-    small = (gbin, ggain, gbias)
     for b in range(4):
         own = slice(128 * b, 128 * b + 128)
         for a in range(32):
-            gwin[4 * a : 4 * a + 4, own] = agf[b % 2, 2 * a + b // 2, 0:4, :]
-        for a in range(3):
-            small[a][:, own] = agf[b % 2, 2 * a + b // 2, 4:5, :]
-        for a in range(2):
-            gb1[a : a + 1, own] = agf[b % 2, 2 * (a + 3) + b // 2, 4:5, :]
-            gb2[a : a + 1, own] = agf[b % 2, 2 * (a + 5) + b // 2, 4:5, :]
+            gwin[4 * a : 4 * a + 4, own] = agf[b % 2, 2 * a + b // 2]
+        tile = agt[b % 2, b // 2]
+        for i, out in enumerate((gbin, ggain, gbias)):
+            out[:, own] = tile[i : i + 1, :]
+        gb1[:, own] = tile[3:5, :]
+        gb2[:, own] = tile[5:7, :]
     for copy in outs:
         copy.wait()
 
@@ -494,11 +549,11 @@
     operands = (
         frames, enc_taps, enc_bias.reshape(1, -1), enc_proj.T, w_in, b_in.reshape(1, -1), ln_gain.reshape(1, -1),
         ln_bias.reshape(1, -1), spec_w1, spec_b1, spec_w2, spec_b2, cotangent) + tuple(jnp.asarray(t) for t in tables())
-    den, agw, agf = pl.pallas_call(
+    den, agw, agf, agt = pl.pallas_call(
         kernel,
-        out_shape=(shape((ROWS, LAT, WIDTH), BF16), shape((2, 32, 2, 8, 128), F32), shape((2, 64, 8, 128), F32)),
+        out_shape=(shape((ROWS, LAT, WIDTH), BF16), shape((2, 32, 2, 8, 128), F32), shape((2, 64, 4, 128), F32), shape((2, 2, 8, 128), F32)),
         in_specs=[hbm] * 20,
-        out_specs=(anywhere, anywhere, anywhere),
+        out_specs=(anywhere,) * 4,
         scratch_shapes=[pltpu.VMEM(x.shape, x.dtype) for x in operands] + [
             pltpu.VMEM((FRAMES, 272, 128), F32),
             pltpu.VMEM((NC, FRAMES, 3, 8, 128), BF16),
@@ -519,19 +574,24 @@
             pltpu.VMEM((4, 8 * ND, 128), F32),
             pltpu.VMEM((4, ND, 8, 512), BF16),
             pltpu.VMEM((4, ND, 8, 512), BF16),
-            pltpu.VMEM((256, 256), F32),
-            pltpu.VMEM((256, 256), F32),
+            pltpu.VMEM((2, 256, 256), BF16),
+            pltpu.VMEM((2, 256, 256), BF16),
             pltpu.VMEM((8, WIDTH), F32),
             pltpu.VMEM((32, 8, 128), F32),
             pltpu.VMEM((32, 8, 128), F32),
             pltpu.VMEM((2, 32, 2, 8, 128), F32),
+            pltpu.VMEM((2, 64, 4, 128), F32),
+            pltpu.VMEM((64, 4, 128), F32),
+            pltpu.VMEM((64, 4, 128), F32),
+            pltpu.VMEM((64, 4, 128), F32),
+            pltpu.VMEM((2, 64, 4, 128), F32),
+            pltpu.VMEM((2, 2, 8, 128), F32),
+            pltpu.VMEM((2, 8, 128), F32),
+            pltpu.VMEM((2, 8, 128), F32),
             pltpu.VMEM((2, 64, 8, 128), F32),
-            pltpu.VMEM((64, 8, 128), F32),
-            pltpu.VMEM((64, 8, 128), F32),
-            pltpu.VMEM((64, 8, 128), F32),
-            pltpu.VMEM((2, 64, 8, 128), F32),
+            pltpu.VMEM((2, 2, 8, 128), F32),
             dma((20,)), dma((8,)), dma(()), dma(()), dma((2,)), dma((2,)), dma((4,)), dma((4,)), dma((4,)),
-            dma(()), dma(()), dma(()), dma(()), dma(()), dma(()), dma(()), dma(()), dma((3,)), dma((3,)),
+            dma(()), dma(()), dma(()), dma(()), dma(()), dma(()), dma(()), dma(()), dma((5,)), dma((5,)), dma((2,)), dma((2,)), dma((2,)), dma((2,)),
         ],
         compiler_params=pltpu.CompilerParams(
             collective_id=0, has_side_effects=True, vmem_limit_bytes=VMEM_LIMIT),
@@ -543,12 +603,12 @@
             shape((ROWS, LAT, WIDTH), BF16), shape((128, WIDTH), F32), shape((1, WIDTH), F32), shape((1, WIDTH), F32),
             shape((1, WIDTH), F32), shape((2, 8, 64, 64), F32), shape((2, WIDTH), F32), shape((2, 8, 64, 64), F32),
             shape((2, WIDTH), F32)),
-        in_specs=[vmem] * 3,
+        in_specs=[vmem] * 4,
         out_specs=(hbm,) + (vmem,) * 8,
         scratch_shapes=[dma((ROWS,))],
         compiler_params=pltpu.CompilerParams(vmem_limit_bytes=16 * 1024 * 1024),
         name="finish",
-    )(den, agw, agf)
+    )(den, agw, agf, agt)
     return (den, gwin, gbin.reshape(-1), ggain.reshape(-1), gbias.reshape(-1), gw1, gb1, gw2, gb2)
 
 

time: 98.6 us -> 92 us (0.933)
  Pallas kernels: 97.6 us -> 91.1 us
    pallas_call x1, Pallas kernels: 95.2 us -> 88.6 us  [body(): pl.pallas_call(kernel, out_shape=(shape((ROWS, LAT, WIDTH), BF16), shape(...]
where the time goes in v3:
time: 92 us; the launch traced here: 91.9 us
  Pallas kernels  91.1 us (99%)
    pallas_call x1, Pallas kernels, body(): pl.pallas_call(kernel, out_shape=(shape((ROWS, LAT, WIDTH), BF16), shape(...  88.6 us
    pallas_call x1, Pallas kernels, body(): pl.pallas_call(finish, out_shape=(shape((ROWS, LAT, WIDTH), BF16), shape(...  2.44 us

profile of v3, /device:TPU:1, one launch (start us, length us, event | category | flops | bytes accessed | tf_op | source)
XLA Modules:
  0.0 91.9 jit_solution(2173461049927339349)
XLA Ops:
  0.6 88.6 %step.1 = (bf16[4,512,512]{2,1,0:T(8,128)(2,1)S(1)}, f32[2,32,2,8,128]{4,3,2,1,0:T(8,128)S(1)}, f32[2,64,4,128]{3,2,1,0:T(4,128)S(1)}, f32[2,2,8,128]{3,2,1,0:T(8,128)S(1)}) custom-call(bf16[4,256,128]{2,1,0:T(8,128)(2,1)} %frames_h.1, f32[9,32]{1,0:T(8,128)} %taps_h.1, f32[1,32]{1,0:T(1,128)} %bitcast.12, bf16[32,512]{1,0:T(8,128)(2,1)} %bitcast.8, ...), custom_call_target="tpu_custom_call" | custom-call | tf_op jit(solution)/shard_map/step/pallas_call | solution.py:552
  89.3 2.4 %finish.1 = (bf16[4,512,512]{2,1,0:T(8,128)(2,1)}, f32[128,512]{1,0:T(8,128)}, f32[1,512]{1,0:T(1,128)}, f32[1,512]{1,0:T(1,128)}, f32[1,512]{1,0:T(1,128)}, /*i...) custom-call(bf16[4,512,512]{2,1,0:T(8,128)(2,1)S(1)} %get-tuple-element.22.den_in, ...), custom_call_target="tpu_custom_call" | custom-call | tf_op jit(solution)/shard_map/finish/pallas_call | solution.py:600

commit v4 on v3

--- a/solution.py
+++ b/solution.py
@@ -32,8 +32,8 @@
 
 
 PEERS = far_first()
-OUT_FIRST = 24
-OUT_SECOND = 24
+OUT_FIRST = 40
+OUT_SECOND = 40
 SUMS_AT = 4
 VMEM_LIMIT = 44 * 1024 * 1024
 EPS = 1e-05
@@ -62,7 +62,7 @@
                 for tap in range(9):
                     place[4 * y + x, 16 * part + tap, 48 * part + 8 * (y + tap // 3) + x + tap % 3] = 1.0
                 place[4 * y + x, 16 * part + 9, 48 * part + 6] = 1.0
-    return wf, wi, np.ascontiguousarray(wf.T), np.ascontiguousarray(wi.T), rot, np.ascontiguousarray(rot.T), place.astype(ml_dtypes.bfloat16)
+    return wf, wi, rot, place.astype(ml_dtypes.bfloat16)
 
 
 def dot(a, b, precision=None):
@@ -83,9 +83,9 @@
 
 def kernel(
     frames_h, taps_h, bias_h, proj_h, w_in_h, b_in_h, gain_h, lbias_h, w1_h, b1_h, w2_h, b2_h, cot_h,
-    wf_h, wi_h, wft_h, wit_h, rot_h, rott_h, place_h,
+    wf_h, wi_h, rot_h, place_h,
     den_hbm, agw_out, agf_out, agt_out,
-    frames, taps, bias, proj, w_in, b_in, gain, lbias, w1, b1, w2, b2, cot, wf, wi, wft, wit, rot, rott, place,
+    frames, taps, bias, proj, w_in, b_in, gain, lbias, w1, b1, w2, b2, cot, wf, wi, rot, place, wft, wit, rott,
     ft, fsend, htop, hbot, frecv, rtop, rbot, est, wbig, projt, tp, lat, emb, nrm, istd, den,
     stage, snd, rcv, wc1, wc2, bc, wsend, wrecv, agw, fsnd, fpair, fsum, frcv, agf, tiny, tpair, tsum, trcv, agt,
     isem, lsem, fss, frs, hss, hrs, ass, ars, als, wss, wrs, gss, grs, rss, rrs, qss, qrs, pss, prs, tss, trs, uss, urs,
@@ -116,7 +116,7 @@
     for i, (src, dst) in enumerate((
             (frames_h, frames), (cot_h, cot), (wi_h, wi), (taps_h, taps), (bias_h, bias), (place_h, place), (proj_h, proj),
             (w1_h, w1), (w2_h, w2), (b1_h, b1), (b2_h, b2), (w_in_h, w_in), (b_in_h, b_in), (gain_h, gain),
-            (lbias_h, lbias), (wf_h, wf), (rot_h, rot), (rott_h, rott), (wit_h, wit), (wft_h, wft))):
+            (lbias_h, lbias), (wf_h, wf), (rot_h, rot))):
         inputs[i] = pltpu.make_async_copy(src, dst, isem.at[i])
         inputs[i].start()
 
@@ -179,6 +179,33 @@
     def recv_all(e):
         pltpu.make_async_copy(snd.at[e, me], rcv.at[e, me], als.at[e]).wait()
         batch(rcv.at[e, pl.ds(0, ND - 1)], ass.at[e], ars.at[e]).wait_recv()
+
+    pl.semaphore_wait(barrier, ND - 1)
+
+    for j in [at_col[yh, x, k] for z, yl, yh, x, k in PEERS if z == yl == 0]:
+        remote(fsend.at[j], frecv.at[c], fss, frs, r * NC + j).start()
+
+    own_frames = pltpu.make_async_copy(fsend.at[c], frecv.at[c], lsem.at[1])
+    own_frames.start()
+
+    @pl.when(r < NR - 1)
+    def _():
+        remote(htop, rtop.at[c], hss.at[0], hrs.at[0], (r + 1) * NC).start()
+
+    @pl.when(r > 0)
+    def _():
+        remote(hbot, rbot.at[c], hss.at[1], hrs.at[1], r * NC - 1).start()
+
+    has_top = jnp.logical_and(c == 0, r > 0)
+    has_bot = jnp.logical_and(c == NC - 1, r < NR - 1)
+
+    @pl.when(jnp.logical_not(has_top))
+    def _():
+        rtop[...] = jnp.zeros(rtop.shape, BF16)
+
+    @pl.when(jnp.logical_not(has_bot))
+    def _():
+        rbot[...] = jnp.zeros(rbot.shape, BF16)
 
     arrive(1, 2)
     for h in range(ROWS):
@@ -223,33 +250,13 @@
         for t in range(4):
             est[f, t, pl.ds(6, 24, stride=8), :] = jnp.ones((24, 128), F32)
             est[f, t, pl.ds(7, 24, stride=8), :] = jnp.zeros((24, 128), F32)
-
-    pl.semaphore_wait(barrier, ND - 1)
-
-    for j in [at_col[yh, x, k] for z, yl, yh, x, k in PEERS if z == yl == 0]:
-        remote(fsend.at[j], frecv.at[c], fss, frs, r * NC + j).start()
-
-    own_frames = pltpu.make_async_copy(fsend.at[c], frecv.at[c], lsem.at[1])
-    own_frames.start()
-
-    @pl.when(r < NR - 1)
-    def _():
-        remote(htop, rtop.at[c], hss.at[0], hrs.at[0], (r + 1) * NC).start()
-
-    @pl.when(r > 0)
-    def _():
-        remote(hbot, rbot.at[c], hss.at[1], hrs.at[1], r * NC - 1).start()
-
-    has_top = jnp.logical_and(c == 0, r > 0)
-    has_bot = jnp.logical_and(c == NC - 1, r < NR - 1)
-
-    @pl.when(jnp.logical_not(has_top))
-    def _():
-        rtop[...] = jnp.zeros(rtop.shape, BF16)
-
-    @pl.when(jnp.logical_not(has_bot))
-    def _():
-        rbot[...] = jnp.zeros(rbot.shape, BF16)
+    eye = (row == col).astype(F32).astype(BF16)
+    arrive(15, 16)
+    wft[...] = dot_t(wf[...], eye[0:256, 0:256], ((0,), (0,))).astype(BF16)
+    wit[...] = dot_t(wi[...], eye[0:256, 0:256], ((0,), (0,))).astype(BF16)
+    for i in range(2):
+        own = slice(512 * i, 512 * i + 512)
+        rott[own, :] = dot_t(rot[:, own], eye[0:256, 0:256], ((0,), (0,))).astype(BF16)
 
     send_own(0)
 
@@ -295,7 +302,7 @@
             hidden = jnp.maximum(hidden, 0.0).astype(BF16)
             lat[h, 32 * f : 32 * f + 32, :] = dot(projt[...], hidden).astype(BF16)
 
-    arrive(11, 12, 13, 14, 15)
+    arrive(11, 12, 13, 14)
     for h in range(ROWS):
         embedded = dot_t(lat[h], w_in[...], ((0,), (0,))) + b_in[...]
         emb[h] = embedded
@@ -332,7 +339,6 @@
         dims = ((1,), (side,))
         return dot_t(high, wc[0], dims) + (dot_t(high, wc[1], dims) + dot_t(low, wc[0], dims))
 
-    arrive(16, 17, 18, 19)
     recv_all(0)
     grad = to_modes(0)
     grad_act = dot3(grad, wc2, 1)
@@ -552,9 +558,12 @@
     den, agw, agf, agt = pl.pallas_call(
         kernel,
         out_shape=(shape((ROWS, LAT, WIDTH), BF16), shape((2, 32, 2, 8, 128), F32), shape((2, 64, 4, 128), F32), shape((2, 2, 8, 128), F32)),
-        in_specs=[hbm] * 20,
+        in_specs=[hbm] * 17,
         out_specs=(anywhere,) * 4,
         scratch_shapes=[pltpu.VMEM(x.shape, x.dtype) for x in operands] + [
+            pltpu.VMEM((LAT, 256), BF16),
+            pltpu.VMEM((LAT, 256), BF16),
+            pltpu.VMEM((2 * LAT, 2 * KH), BF16),
             pltpu.VMEM((FRAMES, 272, 128), F32),
             pltpu.VMEM((NC, FRAMES, 3, 8, 128), BF16),
             pltpu.VMEM((FRAMES, 8, 128), BF16),
@@ -590,7 +599,7 @@
             pltpu.VMEM((2, 8, 128), F32),
             pltpu.VMEM((2, 64, 8, 128), F32),
             pltpu.VMEM((2, 2, 8, 128), F32),
-            dma((20,)), dma((8,)), dma(()), dma(()), dma((2,)), dma((2,)), dma((4,)), dma((4,)), dma((4,)),
+            dma((17,)), dma((8,)), dma(()), dma(()), dma((2,)), dma((2,)), dma((4,)), dma((4,)), dma((4,)),
             dma(()), dma(()), dma(()), dma(()), dma(()), dma(()), dma(()), dma(()), dma((5,)), dma((5,)), dma((2,)), dma((2,)), dma((2,)), dma((2,)),
         ],
         compiler_params=pltpu.CompilerParams(

time: 92 us -> 93.1 us (1.012)
  no operation moved by 1% of the time
where the time goes in v4:
time: 93.1 us; the launch traced here: 92.5 us
  Pallas kernels  91.7 us (98%)
    pallas_call x1, Pallas kernels, body(): pl.pallas_call(kernel, out_shape=(shape((ROWS, LAT, WIDTH), BF16), shape(...  89.2 us
    pallas_call x1, Pallas kernels, body(): pl.pallas_call(finish, out_shape=(shape((ROWS, LAT, WIDTH), BF16), shape(...  2.44 us

profile of v4, /device:TPU:1, one launch (start us, length us, event | category | flops | bytes accessed | tf_op | source)
XLA Modules:
  0.0 92.5 jit_solution(322397151020827327)
XLA Ops:
  0.6 89.2 %step.1 = (bf16[4,512,512]{2,1,0:T(8,128)(2,1)S(1)}, f32[2,32,2,8,128]{4,3,2,1,0:T(8,128)S(1)}, f32[2,64,4,128]{3,2,1,0:T(4,128)S(1)}, f32[2,2,8,128]{3,2,1,0:T(8,128)S(1)}) custom-call(bf16[4,256,128]{2,1,0:T(8,128)(2,1)} %frames_h.1, f32[9,32]{1,0:T(8,128)} %taps_h.1, f32[1,32]{1,0:T(1,128)} %bitcast.12, bf16[32,512]{1,0:T(8,128)(2,1)} %bitcast.8, ...), custom_call_target="tpu_custom_call" | custom-call | tf_op jit(solution)/shard_map/step/pallas_call | solution.py:558
  89.9 2.4 %finish.1 = (bf16[4,512,512]{2,1,0:T(8,128)(2,1)}, f32[128,512]{1,0:T(8,128)}, f32[1,512]{1,0:T(1,128)}, f32[1,512]{1,0:T(1,128)}, f32[1,512]{1,0:T(1,128)}, /*i...) custom-call(bf16[4,512,512]{2,1,0:T(8,128)(2,1)S(1)} %get-tuple-element.22.den_in, ...), custom_call_target="tpu_custom_call" | custom-call | tf_op jit(solution)/shard_map/finish/pallas_call | solution.py:609
